TPU v7x, 32 devices: a whole 2x2x4 slice. The times are simulated.
32 devices in a mesh: dp: 8 (over z, y), mod: 4 (over x, core).
Axes of the slice: x: 2, y: 2, z: 4, core: 2. Of those that a mesh axis runs over, the one named last changes fastest.
Arguments:
- text_emb: bfloat16 [64, 384, 768], P(('dp', 'mod')), may hold values from -6 to 6
- feature_maps: bfloat16 [64, 320, 256], P(('dp', 'mod')), may hold values from -6 to 6
- boxes: int32 [64, 128, 4], P(('dp', 'mod')), may hold values from 0 to 16, as said below
- row_counts: int32 [64, 2], P('dp'), may hold values from 1 to 384, as said below
- w_roi: bfloat16 [512, 768], P('dp'), may hold values from -0.25 to 0.25
- bn_gain: bfloat16 [768], P('dp'), may hold values from 0.5 to 1.5
- bn_bias: bfloat16 [768], P('dp'), may hold values from -1.75 to 1.75
- w_query: bfloat16 [768, 768], P('dp'), may hold values from -0.21875 to 0.21875
- w_key: bfloat16 [768, 768], P('dp'), may hold values from -0.21875 to 0.21875
- w_value: bfloat16 [768, 768], P('dp'), may hold values from -0.21875 to 0.21875
- b_query: bfloat16 [768], P('dp'), may hold values from -3 to 3
- b_value: bfloat16 [768], P('dp'), may hold values from -3 to 3
- w_out: bfloat16 [768, 768], P('dp'), may hold values from -0.625 to 0.625
- b_out: bfloat16 [768], P('dp'), may hold values from -3 to 3
- ln1_gain: bfloat16 [768], P('dp'), may hold values from 0.5 to 1.5
- ln1_bias: bfloat16 [768], P('dp'), may hold values from -1.75 to 1.75
- w_up: bfloat16 [768, 3072], P('dp'), may hold values from -0.21875 to 0.21875
- b_up: bfloat16 [3072], P('dp'), may hold values from -3 to 3
- w_down: bfloat16 [3072, 768], P('dp'), may hold values from -0.109375 to 0.109375
- b_down: bfloat16 [768], P('dp'), may hold values from -1.75 to 1.75
- ln2_gain: bfloat16 [768], P('dp'), may hold values from 0.5 to 1.5
- ln2_bias: bfloat16 [768], P('dp'), may hold values from -1.75 to 1.75
- out_grad_text: bfloat16 [64, 384, 768], P(('dp', 'mod')), may hold values from -6 to 6
- out_grad_roi: bfloat16 [64, 128, 768], P(('dp', 'mod')), may hold values from -6 to 6
Outputs:
- out_text: bfloat16 [64, 384, 768], P(('dp', 'mod'))
- out_roi: bfloat16 [64, 128, 768], P(('dp', 'mod'))
- grad_text: float32 [64, 384, 768], P(('dp', 'mod'))
- grad_maps: float32 [64, 320, 256], P(('dp', 'mod'))
- grad_w_roi: float32 [512, 768], P('dp')
- grad_bn_gain: float32 [768], P('dp')
- grad_bn_bias: float32 [768], P('dp')
- grad_w_query: float32 [768, 768], P('dp')
- grad_w_key: float32 [768, 768], P('dp')
- grad_w_value: float32 [768, 768], P('dp')
- grad_b_query: float32 [768], P('dp')
- grad_b_value: float32 [768], P('dp')
- grad_w_out: float32 [768, 768], P('dp')
- grad_b_out: float32 [768], P('dp')
- grad_ln1_gain: float32 [768], P('dp')
- grad_ln1_bias: float32 [768], P('dp')
- grad_w_up: float32 [768, 3072], P('dp')
- grad_b_up: float32 [3072], P('dp')
- grad_w_down: float32 [3072, 768], P('dp')
- grad_b_down: float32 [768], P('dp')
- grad_ln2_gain: float32 [768], P('dp')
- grad_ln2_bias: float32 [768], P('dp')
Inputs may be any that keep to these rules, and one draw needn't show every extreme that they name: `boxes`: each box is x0, y0, x1, y1 on the 16 x 16 fine grid with x0 < x1 and y0 < y1; a box covering the whole grid occurs. `row_counts`: column 0 counts a page's live text rows, at most 384; column 1 its live 128 rows, at most 128; both bounds are reached; live rows are the first slots.
All inputs are finite; a program needn't handle non-finite values.
Results may differ from a plain program's by a relative error of at most 0.022.
Values may be sent and summed in bfloat16 or wider, within the bound.
A program may use at most 256 MiB of HBM per device.

v0:
```python
import jax
import jax.numpy as jnp
from jax import lax
from jax.sharding import PartitionSpec as P

HEADS = 12
FINE = 16
COARSE = 8


def swapped(block, axis, distance):
    count = lax.axis_size(axis)
    route = []
    for low in range(count):
        high = low | 1 << distance
        if high != low and high < count:
            route += [(low, high), (high, low)]
    return lax.ppermute(block, axis, route)


def product(left_mat, right_mat):
    return jnp.dot(left_mat, right_mat, preferred_element_type=jnp.float32)


def inner_rows(left_mat, right_mat):
    return lax.dot_general(
        left_mat, right_mat, (((0,), (0,)), ((), ())), preferred_element_type=jnp.float32
    )


def outer_cols(left_mat, right_mat):
    return lax.dot_general(
        left_mat, right_mat, (((1,), (1,)), ((), ())), preferred_element_type=jnp.float32
    )


def layer_norm(hidden_in, gain_vec, bias_vec):
    average = jnp.mean(hidden_in, axis=-1, keepdims=True)
    centered = hidden_in - average
    variance = jnp.mean(centered * centered, axis=-1, keepdims=True)
    return centered * lax.rsqrt(variance + 1e-05) * gain_vec + bias_vec


def exact_gelu(hidden_in):
    return jax.nn.gelu(hidden_in, approximate=False)


def box_masks(boxes):
    left_edge = boxes[..., 0:1]
    top_edge = boxes[..., 1:2]
    right_edge = boxes[..., 2:3]
    bottom_edge = boxes[..., 3:4]
    fine_cell = jnp.arange(FINE * FINE, dtype=jnp.int32)
    fine_row = fine_cell // FINE
    fine_col = fine_cell % FINE
    inside_fine = (
        (fine_col >= left_edge)
        & (fine_col < right_edge)
        & (fine_row >= top_edge)
        & (fine_row < bottom_edge)
    )
    coarse_cell = jnp.arange(COARSE * COARSE, dtype=jnp.int32)
    coarse_row = coarse_cell // COARSE
    coarse_col = coarse_cell % COARSE
    inside_coarse = (
        (coarse_col >= left_edge // 2)
        & (coarse_col < (right_edge + 1) // 2)
        & (coarse_row >= top_edge // 2)
        & (coarse_row < (bottom_edge + 1) // 2)
    )
    return (inside_coarse, inside_fine)


def masked_scores(query_part, key_part, key_live, score_scale):
    raw_scores = (
        jnp.einsum("pqhe,pkhe->phqk", query_part, key_part, preferred_element_type=jnp.float32)
        * score_scale
    )
    return jnp.where(key_live[:, None, None, :], raw_scores, -1e30)


def attend(query_part, key_part, value_part, key_live, score_scale):
    scores = masked_scores(query_part, key_part, key_live, score_scale)
    highest_score = jnp.max(scores, -1, keepdims=True)
    exponent = jnp.exp(scores - highest_score)
    normalizer = jnp.sum(exponent, -1, keepdims=True)
    weights_soft = exponent / normalizer
    context = jnp.einsum(
        "phqk,pkhe->pqhe",
        weights_soft.astype(jnp.bfloat16),
        value_part,
        preferred_element_type=jnp.float32,
    )
    return (context, highest_score + jnp.log(normalizer))


def attend_back(query_part, key_part, value_part, key_live, logsum, grad_context, score_scale):
    scores = masked_scores(query_part, key_part, key_live, score_scale)
    weights_soft = jnp.exp(scores - logsum)
    grad_weights = jnp.einsum(
        "pqhe,pkhe->phqk", grad_context, value_part, preferred_element_type=jnp.float32
    )
    grad_value = jnp.einsum(
        "phqk,pqhe->pkhe",
        weights_soft.astype(jnp.bfloat16),
        grad_context,
        preferred_element_type=jnp.float32,
    )
    row_delta = jnp.sum(grad_weights * weights_soft, -1, keepdims=True)
    grad_scores = (weights_soft * (grad_weights - row_delta)).astype(jnp.bfloat16)
    grad_query = (
        jnp.einsum("phqk,pkhe->pqhe", grad_scores, key_part, preferred_element_type=jnp.float32)
        * score_scale
    )
    grad_key = (
        jnp.einsum("phqk,pqhe->pkhe", grad_scores, query_part, preferred_element_type=jnp.float32)
        * score_scale
    )
    return (grad_query, grad_key, grad_value)


def key_value(row_data, key_weight, value_weight, value_bias):
    return (
        product(row_data, key_weight).astype(jnp.bfloat16),
        (product(row_data, value_weight) + value_bias).astype(jnp.bfloat16),
    )


def body(
    text_emb,
    feature_maps,
    boxes,
    row_counts,
    w_roi,
    bn_gain,
    bn_bias,
    w_query,
    w_key,
    w_value,
    b_query,
    b_value,
    w_out,
    b_out,
    ln1_gain,
    ln1_bias,
    w_up,
    b_up,
    w_down,
    b_down,
    ln2_gain,
    ln2_bias,
    out_grad_text,
    out_grad_roi,
):
    page_count, text_slots, model_width = text_emb.shape
    roi_slots = boxes.shape[1]
    channels = feature_maps.shape[2]
    head_count = HEADS
    head_size = model_width // head_count
    score_scale = head_size ** (-0.5)
    coarse_cells = COARSE * COARSE
    text_count = page_count * text_slots
    full_params = (
        lax.all_gather(w_roi, "dp", axis=0, tiled=True),
        lax.all_gather(bn_gain, "dp", axis=0, tiled=True),
        lax.all_gather(bn_bias, "dp", axis=0, tiled=True),
        lax.all_gather(w_query, "dp", axis=0, tiled=True),
        lax.all_gather(w_key, "dp", axis=0, tiled=True),
        lax.all_gather(w_value, "dp", axis=0, tiled=True),
        lax.all_gather(b_query, "dp", axis=0, tiled=True),
        lax.all_gather(b_value, "dp", axis=0, tiled=True),
        lax.all_gather(w_out, "dp", axis=0, tiled=True),
        lax.all_gather(b_out, "dp", axis=0, tiled=True),
        lax.all_gather(ln1_gain, "dp", axis=0, tiled=True),
        lax.all_gather(ln1_bias, "dp", axis=0, tiled=True),
        lax.all_gather(w_up, "dp", axis=0, tiled=True),
        lax.all_gather(b_up, "dp", axis=0, tiled=True),
        lax.all_gather(w_down, "dp", axis=0, tiled=True),
        lax.all_gather(b_down, "dp", axis=0, tiled=True),
        lax.all_gather(ln2_gain, "dp", axis=0, tiled=True),
        lax.all_gather(ln2_bias, "dp", axis=0, tiled=True),
    )
    (
        roi_weight,
        norm_gain,
        norm_bias,
        query_weight,
        key_weight,
        value_weight,
        query_bias,
        value_bias,
        out_weight,
        out_bias,
        first_gain,
        first_bias,
        up_weight,
        up_bias,
        down_weight,
        down_bias,
        second_gain,
        second_bias,
    ) = full_params
    (
        norm_gain,
        norm_bias,
        query_bias,
        value_bias,
        out_bias,
        first_gain,
        first_bias,
        up_bias,
        down_bias,
        second_gain,
        second_bias,
    ) = tuple(
        (
            vector.astype(jnp.float32)
            for vector in (
                norm_gain,
                norm_bias,
                query_bias,
                value_bias,
                out_bias,
                first_gain,
                first_bias,
                up_bias,
                down_bias,
                second_gain,
                second_bias,
            )
        )
    )
    mod_size = lax.axis_size("mod")
    top_bit = mod_size.bit_length() - 2
    my_mod = lax.axis_index("mod")
    partner = (my_mod + mod_size // 2) % mod_size
    own_counts = lax.dynamic_slice_in_dim(row_counts, my_mod * page_count, page_count, 0)
    other_counts = lax.dynamic_slice_in_dim(row_counts, partner * page_count, page_count, 0)
    text_index = jnp.arange(text_slots, dtype=jnp.int32)[None, :]
    roi_index = jnp.arange(roi_slots, dtype=jnp.int32)[None, :]
    own_text_live = text_index < own_counts[:, 0:1]
    own_roi_live = roi_index < own_counts[:, 1:2]
    other_text_live = text_index < other_counts[:, 0:1]
    other_roi_live = roi_index < other_counts[:, 1:2]
    row_live = jnp.concatenate([own_text_live.reshape(-1), other_roi_live.reshape(-1)]).astype(
        jnp.float32
    )[:, None]
    roi_mask = other_roi_live.reshape(-1, 1).astype(jnp.float32)
    inside_coarse, inside_fine = box_masks(boxes)
    coarse_area = jnp.sum(inside_coarse.astype(jnp.float32), -1, keepdims=True)
    fine_area = jnp.sum(inside_fine.astype(jnp.float32), -1, keepdims=True)
    coarse_pool = (
        jnp.einsum(
            "prc,pcf->prf",
            inside_coarse.astype(jnp.bfloat16),
            feature_maps[:, :coarse_cells],
            preferred_element_type=jnp.float32,
        )
        / coarse_area
    )
    fine_pool = (
        jnp.einsum(
            "prc,pcf->prf",
            inside_fine.astype(jnp.bfloat16),
            feature_maps[:, coarse_cells:],
            preferred_element_type=jnp.float32,
        )
        / fine_area
    )
    pooled = (
        jnp.concatenate([coarse_pool, fine_pool], -1)
        .astype(jnp.bfloat16)
        .reshape(page_count * roi_slots, 2 * channels)
    )
    projected = product(pooled, roi_weight)
    column_sum, square_sum, number = lax.psum(
        (
            jnp.sum(projected * roi_mask, 0),
            jnp.sum(projected * projected * roi_mask, 0),
            jnp.sum(roi_mask),
        ),
        ("dp", "mod"),
    )
    average = column_sum / number
    variance = square_sum / number - average * average
    inv_std = lax.rsqrt(variance + 1e-05)
    standard = (projected - average) * inv_std
    roi_rows = (standard * norm_gain + norm_bias).astype(jnp.bfloat16)
    text_rows = text_emb.reshape(text_count, model_width)
    text_query = (product(text_rows, query_weight) + query_bias).astype(jnp.bfloat16)
    roi_query = (product(roi_rows, query_weight) + query_bias).astype(jnp.bfloat16)
    text_key, text_value = key_value(text_rows, key_weight, value_weight, value_bias)
    roi_key, roi_value = key_value(roi_rows, key_weight, value_weight, value_bias)
    far_text_key, far_text_value, far_roi_key, far_roi_value = swapped(
        (text_key, text_value, roi_key, roi_value), "mod", top_bit
    )

    def head_view(flat_rows, slot_count):
        return flat_rows.reshape(page_count, slot_count, head_count, head_size)

    query_own = head_view(text_query, text_slots)
    keys_own = jnp.concatenate(
        [head_view(text_key, text_slots), head_view(far_roi_key, roi_slots)], 1
    )
    values_own = jnp.concatenate(
        [head_view(text_value, text_slots), head_view(far_roi_value, roi_slots)], 1
    )
    live_own = jnp.concatenate([own_text_live, own_roi_live], 1)
    query_other = head_view(roi_query, roi_slots)
    keys_other = jnp.concatenate(
        [head_view(far_text_key, text_slots), head_view(roi_key, roi_slots)], 1
    )
    values_other = jnp.concatenate(
        [head_view(far_text_value, text_slots), head_view(roi_value, roi_slots)], 1
    )
    live_other = jnp.concatenate([other_text_live, other_roi_live], 1)
    context_own, logsum_own = attend(query_own, keys_own, values_own, live_own, score_scale)
    context_other, logsum_other = attend(
        query_other, keys_other, values_other, live_other, score_scale
    )
    context = jnp.concatenate(
        [context_own.reshape(-1, model_width), context_other.reshape(-1, model_width)], 0
    ).astype(jnp.bfloat16)
    rows_in = jnp.concatenate([text_rows, roi_rows], 0)
    attended = product(context, out_weight) + out_bias
    normed, first_back = jax.vjp(
        layer_norm, rows_in.astype(jnp.float32) + attended, first_gain, first_bias
    )
    normed_low = normed.astype(jnp.bfloat16)
    hidden = product(normed_low, up_weight) + up_bias
    activated, gelu_back = jax.vjp(exact_gelu, hidden)
    activated_low = activated.astype(jnp.bfloat16)
    second_in = normed + product(activated_low, down_weight) + down_bias
    normed_out, second_back = jax.vjp(layer_norm, second_in, second_gain, second_bias)
    output = normed_out * row_live
    out_text = output[:text_count].reshape(page_count, text_slots, model_width).astype(jnp.bfloat16)
    out_roi = output[text_count:].reshape(page_count, roi_slots, model_width).astype(jnp.bfloat16)
    back_weights = (
        lax.all_gather(w_roi, "dp", axis=0, tiled=True),
        lax.all_gather(w_query, "dp", axis=0, tiled=True),
        lax.all_gather(w_key, "dp", axis=0, tiled=True),
        lax.all_gather(w_value, "dp", axis=0, tiled=True),
        lax.all_gather(w_out, "dp", axis=0, tiled=True),
        lax.all_gather(w_up, "dp", axis=0, tiled=True),
        lax.all_gather(w_down, "dp", axis=0, tiled=True),
    )
    roi_weight, query_weight, key_weight, value_weight, out_weight, up_weight, down_weight = (
        back_weights
    )
    upstream = (
        jnp.concatenate(
            [out_grad_text.reshape(-1, model_width), out_grad_roi.reshape(-1, model_width)], 0
        ).astype(jnp.float32)
        * row_live
    )
    grad_second, grad_ln2_gain, grad_ln2_bias = second_back(upstream)
    grad_mixed = grad_second.astype(jnp.bfloat16)
    grad_w_down = inner_rows(activated_low, grad_mixed)
    grad_b_down = jnp.sum(grad_mixed.astype(jnp.float32), 0)
    (grad_gelu,) = gelu_back(outer_cols(grad_mixed, down_weight))
    grad_hidden = grad_gelu.astype(jnp.bfloat16)
    grad_w_up = inner_rows(normed_low, grad_hidden)
    grad_b_up = jnp.sum(grad_hidden.astype(jnp.float32), 0)
    grad_first, grad_ln1_gain, grad_ln1_bias = first_back(
        grad_second + outer_cols(grad_hidden, up_weight)
    )
    grad_attended = grad_first.astype(jnp.bfloat16)
    grad_w_out = inner_rows(context, grad_attended)
    grad_b_out = jnp.sum(grad_attended.astype(jnp.float32), 0)
    grad_context = outer_cols(grad_attended, out_weight).astype(jnp.bfloat16)
    grad_query_own, grad_key_own, grad_value_own = attend_back(
        query_own,
        keys_own,
        values_own,
        live_own,
        logsum_own,
        head_view(grad_context[:text_count], text_slots),
        score_scale,
    )
    grad_query_other, grad_key_other, grad_value_other = attend_back(
        query_other,
        keys_other,
        values_other,
        live_other,
        logsum_other,
        head_view(grad_context[text_count:], roi_slots),
        score_scale,
    )
    back_roi_key, back_roi_value, back_text_key, back_text_value = (
        swapped(
            grad_key_own[:, text_slots:]
            .reshape(page_count, roi_slots, model_width)
            .astype(jnp.bfloat16),
            "mod",
            top_bit,
        ).astype(jnp.float32),
        swapped(
            grad_value_own[:, text_slots:]
            .reshape(page_count, roi_slots, model_width)
            .astype(jnp.bfloat16),
            "mod",
            top_bit,
        ).astype(jnp.float32),
        swapped(
            grad_key_other[:, :text_slots]
            .reshape(page_count, text_slots, model_width)
            .astype(jnp.bfloat16),
            "mod",
            top_bit,
        ).astype(jnp.float32),
        swapped(
            grad_value_other[:, :text_slots]
            .reshape(page_count, text_slots, model_width)
            .astype(jnp.bfloat16),
            "mod",
            top_bit,
        ).astype(jnp.float32),
    )
    key_text = (
        grad_key_own[:, :text_slots].reshape(page_count, text_slots, model_width) + back_text_key
    )
    value_text = (
        grad_value_own[:, :text_slots].reshape(page_count, text_slots, model_width)
        + back_text_value
    )
    key_roi = (
        grad_key_other[:, text_slots:].reshape(page_count, roi_slots, model_width) + back_roi_key
    )
    value_roi = (
        grad_value_other[:, text_slots:].reshape(page_count, roi_slots, model_width)
        + back_roi_value
    )
    grad_keys = jnp.concatenate(
        [key_text.reshape(-1, model_width), key_roi.reshape(-1, model_width)], 0
    ).astype(jnp.bfloat16)
    grad_values = jnp.concatenate(
        [value_text.reshape(-1, model_width), value_roi.reshape(-1, model_width)], 0
    ).astype(jnp.bfloat16)
    grad_queries = jnp.concatenate(
        [grad_query_own.reshape(-1, model_width), grad_query_other.reshape(-1, model_width)], 0
    ).astype(jnp.bfloat16)
    grad_w_query = inner_rows(rows_in, grad_queries)
    grad_b_query = jnp.sum(grad_queries.astype(jnp.float32), 0)
    grad_w_key = inner_rows(rows_in, grad_keys)
    grad_w_value = inner_rows(rows_in, grad_values)
    grad_b_value = jnp.sum(grad_values.astype(jnp.float32), 0)
    grad_rows = (
        grad_first
        + outer_cols(grad_queries, query_weight)
        + outer_cols(grad_keys, key_weight)
        + outer_cols(grad_values, value_weight)
    )
    grad_text = grad_rows[:text_count].reshape(page_count, text_slots, model_width)
    grad_roi = grad_rows[text_count:]
    sum_grad, sum_scaled = lax.psum(
        (jnp.sum(grad_roi, 0), jnp.sum(grad_roi * standard, 0)), ("dp", "mod")
    )
    grad_projected = (
        inv_std
        * (
            grad_roi * norm_gain
            - roi_mask * norm_gain * (sum_grad + standard * sum_scaled) / number
        )
    ).astype(jnp.bfloat16)
    grad_w_roi = inner_rows(pooled, grad_projected)
    grad_pooled = (
        outer_cols(grad_projected, roi_weight)
        .astype(jnp.bfloat16)
        .astype(jnp.float32)
        .reshape(page_count, roi_slots, 2 * channels)
    )
    grad_coarse = jnp.einsum(
        "prc,prf->pcf",
        inside_coarse.astype(jnp.float32),
        grad_pooled[..., :channels] / coarse_area,
        precision=lax.Precision.HIGHEST,
        preferred_element_type=jnp.float32,
    )
    grad_fine = jnp.einsum(
        "prc,prf->pcf",
        inside_fine.astype(jnp.float32),
        grad_pooled[..., channels:] / fine_area,
        precision=lax.Precision.HIGHEST,
        preferred_element_type=jnp.float32,
    )
    grad_maps = jnp.concatenate([grad_coarse, grad_fine], 1)
    local_grads = (
        grad_w_roi,
        grad_w_query,
        grad_w_key,
        grad_w_value,
        grad_b_query,
        grad_b_value,
        grad_w_out,
        grad_b_out,
        grad_ln1_gain,
        grad_ln1_bias,
        grad_w_up,
        grad_b_up,
        grad_w_down,
        grad_b_down,
        grad_ln2_gain,
        grad_ln2_bias,
    )
    shares = (
        lax.psum_scatter(
            local_grads[0].astype(jnp.bfloat16), "dp", scatter_dimension=0, tiled=True
        ).astype(jnp.float32),
        lax.psum_scatter(
            local_grads[1].astype(jnp.bfloat16), "dp", scatter_dimension=0, tiled=True
        ).astype(jnp.float32),
        lax.psum_scatter(
            local_grads[2].astype(jnp.bfloat16), "dp", scatter_dimension=0, tiled=True
        ).astype(jnp.float32),
        lax.psum_scatter(
            local_grads[3].astype(jnp.bfloat16), "dp", scatter_dimension=0, tiled=True
        ).astype(jnp.float32),
        lax.psum_scatter(
            local_grads[4].astype(jnp.bfloat16), "dp", scatter_dimension=0, tiled=True
        ).astype(jnp.float32),
        lax.psum_scatter(
            local_grads[5].astype(jnp.bfloat16), "dp", scatter_dimension=0, tiled=True
        ).astype(jnp.float32),
        lax.psum_scatter(
            local_grads[6].astype(jnp.bfloat16), "dp", scatter_dimension=0, tiled=True
        ).astype(jnp.float32),
        lax.psum_scatter(
            local_grads[7].astype(jnp.bfloat16), "dp", scatter_dimension=0, tiled=True
        ).astype(jnp.float32),
        lax.psum_scatter(
            local_grads[8].astype(jnp.bfloat16), "dp", scatter_dimension=0, tiled=True
        ).astype(jnp.float32),
        lax.psum_scatter(
            local_grads[9].astype(jnp.bfloat16), "dp", scatter_dimension=0, tiled=True
        ).astype(jnp.float32),
        lax.psum_scatter(
            local_grads[10].astype(jnp.bfloat16), "dp", scatter_dimension=0, tiled=True
        ).astype(jnp.float32),
        lax.psum_scatter(
            local_grads[11].astype(jnp.bfloat16), "dp", scatter_dimension=0, tiled=True
        ).astype(jnp.float32),
        lax.psum_scatter(
            local_grads[12].astype(jnp.bfloat16), "dp", scatter_dimension=0, tiled=True
        ).astype(jnp.float32),
        lax.psum_scatter(
            local_grads[13].astype(jnp.bfloat16), "dp", scatter_dimension=0, tiled=True
        ).astype(jnp.float32),
        lax.psum_scatter(
            local_grads[14].astype(jnp.bfloat16), "dp", scatter_dimension=0, tiled=True
        ).astype(jnp.float32),
        lax.psum_scatter(
            local_grads[15].astype(jnp.bfloat16), "dp", scatter_dimension=0, tiled=True
        ).astype(jnp.float32),
    )
    summed = (
        lax.psum(shares[0].astype(jnp.bfloat16), "mod").astype(jnp.float32),
        lax.psum(shares[1].astype(jnp.bfloat16), "mod").astype(jnp.float32),
        lax.psum(shares[2].astype(jnp.bfloat16), "mod").astype(jnp.float32),
        lax.psum(shares[3].astype(jnp.bfloat16), "mod").astype(jnp.float32),
        lax.psum(shares[4].astype(jnp.bfloat16), "mod").astype(jnp.float32),
        lax.psum(shares[5].astype(jnp.bfloat16), "mod").astype(jnp.float32),
        lax.psum(shares[6].astype(jnp.bfloat16), "mod").astype(jnp.float32),
        lax.psum(shares[7].astype(jnp.bfloat16), "mod").astype(jnp.float32),
        lax.psum(shares[8].astype(jnp.bfloat16), "mod").astype(jnp.float32),
        lax.psum(shares[9].astype(jnp.bfloat16), "mod").astype(jnp.float32),
        lax.psum(shares[10].astype(jnp.bfloat16), "mod").astype(jnp.float32),
        lax.psum(shares[11].astype(jnp.bfloat16), "mod").astype(jnp.float32),
        lax.psum(shares[12].astype(jnp.bfloat16), "mod").astype(jnp.float32),
        lax.psum(shares[13].astype(jnp.bfloat16), "mod").astype(jnp.float32),
        lax.psum(shares[14].astype(jnp.bfloat16), "mod").astype(jnp.float32),
        lax.psum(shares[15].astype(jnp.bfloat16), "mod").astype(jnp.float32),
    )
    share_len = model_width // lax.axis_size("dp")
    share_start = lax.axis_index("dp") * share_len
    gain_share = lax.dynamic_slice_in_dim(sum_scaled, share_start, share_len, 0)
    bias_share = lax.dynamic_slice_in_dim(sum_grad, share_start, share_len, 0)
    return (
        out_text,
        out_roi,
        grad_text,
        grad_maps,
        summed[0],
        gain_share,
        bias_share,
        summed[1],
        summed[2],
        summed[3],
        summed[4],
        summed[5],
        summed[6],
        summed[7],
        summed[8],
        summed[9],
        summed[10],
        summed[11],
        summed[12],
        summed[13],
        summed[14],
        summed[15],
    )


def solution(mesh):
    in_specs = (
        P(("dp", "mod"), None, None),
        P(("dp", "mod"), None, None),
        P(("dp", "mod"), None, None),
        P("dp", None),
        P("dp", None),
        P("dp"),
        P("dp"),
        P("dp", None),
        P("dp", None),
        P("dp", None),
        P("dp"),
        P("dp"),
        P("dp", None),
        P("dp"),
        P("dp"),
        P("dp"),
        P("dp", None),
        P("dp"),
        P("dp", None),
        P("dp"),
        P("dp"),
        P("dp"),
        P(("dp", "mod"), None, None),
        P(("dp", "mod"), None, None),
    )
    out_specs = (
        P(("dp", "mod"), None, None),
        P(("dp", "mod"), None, None),
        P(("dp", "mod"), None, None),
        P(("dp", "mod"), None, None),
        P("dp", None),
        P("dp"),
        P("dp"),
        P("dp", None),
        P("dp", None),
        P("dp", None),
        P("dp"),
        P("dp"),
        P("dp", None),
        P("dp"),
        P("dp"),
        P("dp"),
        P("dp", None),
        P("dp"),
        P("dp", None),
        P("dp"),
        P("dp"),
        P("dp"),
    )
    return jax.shard_map(body, mesh=mesh, in_specs=in_specs, out_specs=out_specs, check_vma=False)
```

profile of v0, /device:TPU:0, one launch (start us, length us, event | category | flops | bytes accessed | tf_op | source)
XLA Modules:
  0.0 1045.8 jit_solution(607304071477233184)
XLA Ops:
  23.3 39.2 %all-reduce.22 = (bf16[768]{0:T(1024)(128)(2,1)S(1)}, bf16[768]{0:T(1024)(128)(2,1)S(1)}, bf16[768]{0:T(1024)(128)(2,1)S(1)}, bf16[768]{0:T(1024)(128)(2,1)S(1)}...) all-reduce(bf16[768]{0:T(1024)(128)(2,1)S(1)} %dynamic-update-slice, ...), channel_id=1, replica_groups=mesh['dp'=8,'mod'=4] {'dp'}, use_global_device_ids=true, to_apply=%add.2 | all-reduce | flops 6912 | bytes 27648
  65.3 26.3 %all-gather = bf16[8,1,384]{2,1,0:T(2,128)(2,1)S(1)} all-gather(bf16[1,1,384]{2,1,0:T(2,128)(2,1)S(1)} %reshape.411), channel_id=1, replica_groups=mesh['dp'=8,'mod'=4] {'dp'}, dimensions={0}, use_global_device_ids=true | all-gather | bytes 6912 | tf_op jit(solution)/shard_map/all_gather | solution.py:177
  95.2 32.5 %all_gather.61 = bf16[512,768]{1,0:T(8,128)(2,1)S(1)} all-gather(bf16[64,768]{1,0:T(8,128)(2,1)S(1)} %copy-done.59), channel_id=1, replica_groups=mesh['dp'=8,'mod'=4] {'dp'}, dimensions={0}, use_global_device_ids=true | all-gather | bytes 884736 | tf_op jit(solution)/shard_map/all_gather | solution.py:164
  129.1 37.4 %all-reduce.20 = (f32[768]{0:T(1024)S(1)}, f32[]{:T(128)}, f32[768]{0:T(1024)S(1)}) all-reduce(f32[768]{0:T(1024)S(1)} %get-tuple-element.31, f32[]{:T(128)} %convert_reduce_fusion.2, f32[768]{0:T(1024)S(1)} %get-tuple-element.30), channel_id=1, replica_groups=mesh['dp'=8,'mod'=4] {'dp','mod'}, use_global_device_ids=true, to_apply=%region_7.8 | all-reduce | flops 1537 | bytes 12296 | tf_op jit(solution)/shard_map/psum | solution.py:276
  236.2 7.0 fusion.29
  266.5 36.1 %multiply_convert_fusion.1 = (bf16[1024,3072]{1,0:T(8,128)(2,1)}, f32[1024,3072]{1,0:T(8,128)}, f32[1024,3072]{1,0:T(8,128)}) fusion(f32[3072]{0:T(1024)S(1)} %bitcast.191, bf16[768,3072]{1,0:T(8,128)(2,1)} %all-gather.16.cloned.1.call-done, f32[1024,768]{1,0:T(8,128)S(1)} %get-tuple-element.113, f32[768]{0:T(1024)S(1)} %copy-done.92, ...), kind=kOutput, calls=%fused_computation.11 | convolution fusion | flops 5043388416 | bytes 39348224 | tf_op jit(solution)/shard_map/dot_general | solution.py:22
  302.6 40.1 %all-gather.18.cloned.1.call-done = bf16[3072,768]{1,0:T(8,128)(2,1)} async-done(((bf16[384,768]{1,0:T(8,128)(2,1)}), bf16[3072,768]{1,0:T(8,128)(2,1)}) %all-gather.18.cloned.1.call-update) | async-done | bytes 4718608 | tf_op jit(solution)/shard_map/all_gather | solution.py:178
  342.7 8.8 fusion.85
  361.0 18.9 %fusion.88 = (bf16[3072]{0:T(1024)(128)(2,1)}, bf16[1024,3072]{1,0:T(8,128)(2,1)}) fusion(f32[1024,3072]{1,0:T(8,128)} %get-tuple-element.85, bf16[1024,768]{1,0:T(8,128)(2,1)} %get-tuple-element.73, bf16[3072,768]{1,0:T(8,128)(2,1)} %all-gather.18.cloned.1.call-done, f32[1024,3072]{1,0:T(8,128)} %get-tuple-element.114, f32[3072]{0:T(1024)S(1)} %bitcast.192), kind=kOutput, calls=%fused_computation.232 | convolution fusion | flops 4882166784 | bytes 37767168 | tf_op jit(solution)/shard_map/dot_general | solution.py:32
  380.0 10.1 multiply_reduce_fusion.3
  420.1 10.0 fusion.22
  430.1 17.6 %multiply_reduce_fusion = (f32[2,12,384]{2,1,0:T(8,128)}, f32[2,12,384,512]{3,2,1,0:T(8,128)}) fusion(f32[2,12,384]{2,1,0:T(8,128)S(1)} %copy-done.48, f32[2,12,384,512]{3,2,1,0:T(8,128)} %copy-done, pred[2,512]{1,0:T(4,128)(4,1)S(1)} %copy-done.58, bf16[2,512,12,64]{1,3,2,0:T(8,128)(2,1)S(1)} %copy-done.23, bf16[2,384,12,64]{1,0,3,2:T(2,128)(2,1)S(1)} %copy-done.26), kind=kOutput, calls=%fused_computation.2 | convolution fusion | flops 627563520 | bytes 40576000 | tf_op jit(solution)/shard_map/pqhe,pkhe->phqk/dot_general | solution.py:100
  465.5 13.6 %multiply_convert_fusion = bf16[2,12,384,512]{3,2,1,0:T(8,128)(2,1)S(1)} fusion(f32[2,12,384,512]{3,2,1,0:T(8,128)} %get-tuple-element.119, f32[2,12,384]{2,1,0:T(8,128)S(1)} %copy-done.52, f32[2,12,384]{2,1,0:T(8,128)S(1)} %copy-done.49, f32[2,12,384,512]{3,2,1,0:T(8,128)} %copy-done, pred[2,512]{1,0:T(4,128)(4,1)S(1)} %copy-done.58), kind=kLoop, calls=%fused_computation.1 | loop fusion | flops 28311552 | bytes 47260672 | tf_op jit(solution)/shard_map/convert_element_type | solution.py:110
  484.6 7.9 fusion.86
  530.9 39.2 %all-reduce.19 = (f32[768]{0:T(1024)}, f32[768]{0:T(1024)}) all-reduce(f32[768]{0:T(1024)S(1)} %get-tuple-element.28, f32[768]{0:T(1024)S(1)} %get-tuple-element.27), channel_id=1, replica_groups=mesh['dp'=8,'mod'=4] {'dp','mod'}, use_global_device_ids=true, to_apply=%region_25.26 | all-reduce | flops 1536 | bytes 12288 | tf_op jit(solution)/shard_map/psum | solution.py:455
  583.6 9.9 convolution_convert_fusion.1
  594.9 10.1 convolution_convert_fusion
  612.4 38.6 %all-reduce.21 = (bf16[768]{0:T(1024)(128)(2,1)}, bf16[768]{0:T(1024)(128)(2,1)}, bf16[768]{0:T(1024)(128)(2,1)}, bf16[768]{0:T(1024)(128)(2,1)}, bf16[768]{0:T(...) all-reduce(bf16[768]{0:T(1024)(128)(2,1)} %dynamic-update-slice.9, ...), channel_id=1, replica_groups=mesh['dp'=8,'mod'=4] {'dp'}, use_global_device_ids=true, to_apply=%add.9 | all-reduce | flops 9984 | bytes 39936
  652.3 59.9 %reduce-scatter.14.cloned.1.call-done = bf16[96,768]{1,0:T(8,128)(2,1)} async-done(((bf16[768,768]{1,0:T(8,128)(2,1)}), bf16[96,768]{1,0:T(8,128)(2,1)}) %reduce-scatter.14.cloned.1.call-update) | async-done | bytes 147472 | tf_op jit(solution)/shard_map/reduce_scatter | solution.py:515
  712.2 67.7 %reduce-scatter.12.cloned.1.call-done = bf16[96,768]{1,0:T(8,128)(2,1)} async-done(((bf16[768,768]{1,0:T(8,128)(2,1)}), bf16[96,768]{1,0:T(8,128)(2,1)}) %reduce-scatter.12.cloned.1.call-update) | async-done | bytes 147472 | tf_op jit(solution)/shard_map/reduce_scatter | solution.py:512
  779.9 98.2 %reduce-scatter.18.cloned.1.call-done = bf16[96,3072]{1,0:T(8,128)(2,1)} async-done(((bf16[768,3072]{1,0:T(8,128)(2,1)}), bf16[96,3072]{1,0:T(8,128)(2,1)}) %reduce-scatter.18.cloned.1.call-update) | async-done | bytes 589840 | tf_op jit(solution)/shard_map/reduce_scatter | solution.py:536
  878.1 99.0 %reduce-scatter.20.cloned.1.call-done = bf16[384,768]{1,0:T(8,128)(2,1)} async-done(((bf16[3072,768]{1,0:T(8,128)(2,1)}), bf16[384,768]{1,0:T(8,128)(2,1)}) %reduce-scatter.20.cloned.1.call-update) | async-done | bytes 589840 | tf_op jit(solution)/shard_map/reduce_scatter | solution.py:542
  991.8 7.4 all-reduce.23
  1006.1 21.5 %all-reduce.27.cloned.1.call-done = (bf16[64,768]{1,0:T(8,128)(2,1)}, bf16[96,768]{1,0:T(8,128)(2,1)}, bf16[96,768]{1,0:T(8,128)(2,1)}, bf16[96,768]{1,0:T(8,128...) async-done(((bf16[64,768]{1,0:T(8,128)(2,1)}, bf16[96,768]{1,0:T(8,128)(2,1)}, bf16[96,768]{1,0:T(8,128)(2,1)}, ...) | async-done | bytes 1867792 | tf_op jit(solution)/shard_map/psum | solution.py:556
  (494 shorter events, 270.6 us)
Async XLA Ops:
  7.2 160.2 %all-gather.12.cloned.1.call-start = ((), (), s32[]{:S(2)}) async-start(), calls=%async_computation.9 | async-start | bytes 1327104 | tf_op jit(solution)/shard_map/all_gather | solution.py:168
  7.9 167.0 %all-gather.8.cloned.1.call-start = ((), (), s32[]{:S(2)}) async-start(), calls=%async_computation.7 | async-start | bytes 1327104 | tf_op jit(solution)/shard_map/all_gather | solution.py:169
  8.7 179.8 %all-gather.10.cloned.1.call-start = ((), (), s32[]{:S(2)}) async-start(), calls=%async_computation.8 | async-start | bytes 1327104 | tf_op jit(solution)/shard_map/all_gather | solution.py:167
  9.4 252.6 %all-gather.14.cloned.1.call-start = ((), (), s32[]{:S(2)}) async-start(), calls=%async_computation.10 | async-start | bytes 1327104 | tf_op jit(solution)/shard_map/all_gather | solution.py:172
  10.0 256.3 %all-gather.16.cloned.1.call-start = ((), (), s32[]{:S(2)}) async-start(), calls=%async_computation.11 | async-start | bytes 5308416 | tf_op jit(solution)/shard_map/all_gather | solution.py:176
  10.6 332.1 %all-gather.18.cloned.1.call-start = ((), (), s32[]{:S(2)}) async-start(), calls=%async_computation.12 | async-start | bytes 5308416 | tf_op jit(solution)/shard_map/all_gather | solution.py:178
  11.2 641.1 %reduce-scatter.16.cloned.1.call-start = ((), (), s32[]{:S(2)}) async-start(), calls=%async_computation.17 | async-start | bytes 1327104 | tf_op jit(solution)/shard_map/reduce_scatter | solution.py:524
  172.6 73.9 %collective-permute-start.3 = (bf16[768,768]{1,0:T(8,128)(2,1)}, bf16[768,768]{1,0:T(8,128)(2,1)}, u32[]{:S(2)}, u32[]{:S(2)}) collective-permute-start(bf16[768,768]{1,0:T(8,128)(2,1)} %convolution_convert_fusion.7), channel_id=1, source_target_pairs={{0,2},{2,0},{1,3},{3,1},{4,6},{6,4},{5,7},{7,5},{8,10},{10,8},{9,1... | collective-permute-start | bytes 3538952 | tf_op jit(solution)/shard_map/ppermute | solution.py:18
  177.4 33.1 %collective-permute-start = (bf16[256,768]{1,0:T(8,128)(2,1)}, bf16[256,768]{1,0:T(8,128)(2,1)}, u32[]{:S(2)}, u32[]{:S(2)}) collective-permute-start(bf16[256,768]{1,0:T(8,128)(2,1)} %fusion.31), channel_id=1, source_target_pairs={{0,2},{2,0},{1,3},{3,1},{4,6},{6,4},{5,7},{7,5},{8,10},{10,8},{9,1... | collective-permute-start | bytes 1179656 | tf_op jit(solution)/shard_map/ppermute | solution.py:18
  180.0 38.9 %collective-permute-start.1 = (bf16[256,768]{1,0:T(8,128)(2,1)}, bf16[256,768]{1,0:T(8,128)(2,1)}, u32[]{:S(2)}, u32[]{:S(2)}) collective-permute-start(bf16[256,768]{1,0:T(8,128)(2,1)} %convolution_convert_fusion.9), channel_id=1, source_target_pairs={{0,2},{2,0},{1,3},{3,1},{4,6},{6,4},{5,7},{7,5},{8,10},{10,8},{9,1... | collective-permute-start | bytes 1179656 | tf_op jit(solution)/shard_map/ppermute | solution.py:18
  188.4 60.1 %collective-permute-start.2 = (bf16[768,768]{1,0:T(8,128)(2,1)}, bf16[768,768]{1,0:T(8,128)(2,1)}, u32[]{:S(2)}, u32[]{:S(2)}) collective-permute-start(bf16[768,768]{1,0:T(8,128)(2,1)} %add_convert_fusion.6), channel_id=1, source_target_pairs={{0,2},{2,0},{1,3},{3,1},{4,6},{6,4},{5,7},{7,5},{8,10},{10,8},{9,1... | collective-permute-start | bytes 3538952 | tf_op jit(solution)/shard_map/ppermute | solution.py:18
  447.7 204.6 %reduce-scatter.10.cloned.1.call-start = ((), (), s32[]{:S(2)}) async-start(), calls=%async_computation.14 | async-start | bytes 1327104 | tf_op jit(solution)/shard_map/reduce_scatter | solution.py:509
  453.3 72.1 %collective-permute-start.6 = (bf16[2,384,768]{2,1,0:T(8,128)(2,1)}, bf16[2,384,768]{2,1,0:T(8,128)(2,1)}, u32[]{:S(2)}, u32[]{:S(2)}) collective-permute-start(bf16[2,384,768]{2,1,0:T(8,128)(2,1)} %copy.141), channel_id=1, source_target_pairs={{0,2},{2,0},{1,3},{3,1},{4,6},{6,4},{5,7},{7,5},{8,10},{10,8},{9,1... | collective-permute-start | bytes 3538952 | tf_op jit(solution)/shard_map/ppermute | solution.py:18
  458.7 56.9 %collective-permute-start.7 = (bf16[2,128,768]{2,1,0:T(8,128)(2,1)}, bf16[2,128,768]{2,1,0:T(8,128)(2,1)}, u32[]{:S(2)}, u32[]{:S(2)}) collective-permute-start(bf16[2,128,768]{2,1,0:T(8,128)(2,1)} %copy.143), channel_id=1, source_target_pairs={{0,2},{2,0},{1,3},{3,1},{4,6},{6,4},{5,7},{7,5},{8,10},{10,8},{9,1... | collective-permute-start | bytes 1179656 | tf_op jit(solution)/shard_map/ppermute | solution.py:18
  464.0 58.1 %collective-permute-start.4 = (bf16[2,384,768]{2,1,0:T(8,128)(2,1)}, bf16[2,384,768]{2,1,0:T(8,128)(2,1)}, u32[]{:S(2)}, u32[]{:S(2)}) collective-permute-start(bf16[2,384,768]{2,1,0:T(8,128)(2,1)} %copy.135), channel_id=1, source_target_pairs={{0,2},{2,0},{1,3},{3,1},{4,6},{6,4},{5,7},{7,5},{8,10},{10,8},{9,1... | collective-permute-start | bytes 3538952 | tf_op jit(solution)/shard_map/ppermute | solution.py:18
  484.0 38.0 %collective-permute-start.5 = (bf16[2,128,768]{2,1,0:T(8,128)(2,1)}, bf16[2,128,768]{2,1,0:T(8,128)(2,1)S(1)}, u32[]{:S(2)}, u32[]{:S(2)}) collective-permute-start(bf16[2,128,768]{2,1,0:T(8,128)(2,1)} %copy.137), channel_id=1, source_target_pairs={{0,2},{2,0},{1,3},{3,1},{4,6},{6,4},{5,7},{7,5},{8,10},{10,8},{9,1... | collective-permute-start | bytes 1179656 | tf_op jit(solution)/shard_map/ppermute | solution.py:18
  497.8 154.5 %reduce-scatter.8.cloned.1.call-start = ((), (), s32[]{:S(2)}) async-start(), calls=%async_computation.13 | async-start | bytes 884736 | tf_op jit(solution)/shard_map/reduce_scatter | solution.py:506
  574.5 137.7 %reduce-scatter.14.cloned.1.call-start = ((), (), s32[]{:S(2)}) async-start(), calls=%async_computation.16 | async-start | bytes 1327104 | tf_op jit(solution)/shard_map/reduce_scatter | solution.py:515
  578.9 200.9 %reduce-scatter.12.cloned.1.call-start = ((), (), s32[]{:S(2)}) async-start(), calls=%async_computation.15 | async-start | bytes 1327104 | tf_op jit(solution)/shard_map/reduce_scatter | solution.py:512
  583.5 294.6 %reduce-scatter.18.cloned.1.call-start = ((), (), s32[]{:S(2)}) async-start(), calls=%async_computation.18 | async-start | bytes 5308416 | tf_op jit(solution)/shard_map/reduce_scatter | solution.py:536
  593.5 383.7 %reduce-scatter.20.cloned.1.call-start = ((), (), s32[]{:S(2)}) async-start(), calls=%async_computation.19 | async-start | bytes 5308416 | tf_op jit(solution)/shard_map/reduce_scatter | solution.py:542
  604.9 372.3 %copy-start.67 = (f32[1024]{0:T(1024)S(1)}, f32[1024]{0:T(1024)}, u32[]{:S(2)}) copy-start(f32[1024]{0:T(1024)} %add_convert_fusion.10) | copy-start | bytes 12292
  605.0 372.3 %copy-start.69 = (f32[1024]{0:T(1024)S(1)}, f32[1024]{0:T(1024)}, u32[]{:S(2)}) copy-start(f32[1024]{0:T(1024)} %copy-done.68) | copy-start | bytes 12292
  605.0 422.6 %all-reduce.27.cloned.1.call-start = ((), (), s32[]{:S(2)}) async-start(), calls=%async_computation.20 | async-start | bytes 3735552 | tf_op jit(solution)/shard_map/psum | solution.py:556
  (118 other events, 4751.5 us)
Sparse Core Ops, SparseCore 0:
  10.2 44.1 all-gather.11
  56.6 42.5 all-gather.7
  101.4 39.5 all-gather.9
  143.0 39.7 all-gather.13
  184.8 78.0 all-gather.15
  264.9 77.7 all-gather.17
  447.8 63.1 reduce-scatter.15
  515.0 63.7 reduce-scatter.9
  582.1 62.2 reduce-scatter.7
  648.3 63.8 reduce-scatter.13
  716.2 63.6 reduce-scatter.11
  783.4 94.7 reduce-scatter.17
  881.8 95.3 reduce-scatter.19
  979.9 47.6 all-reduce.26
where the time goes:
time: 1050 us
  waiting for transfers between devices  399 us (38%)
  blocking collectives  221 us (21%)
  matrix products  207 us (20%)
  local copies, waits for them, and re-layouts  120 us (11%)
  other arithmetic  71.5 us (7%)
  between operations  18.3 us (2%)
    reduce_scatter x1, waiting for transfers between devices, body(): lax.psum_scatter(local_grads[12].astype(jnp.bfloat16), 'dp', scatter_dime...  99 us
    reduce_scatter x1, waiting for transfers between devices, body(): lax.psum_scatter(local_grads[10].astype(jnp.bfloat16), 'dp', scatter_dime...  98.2 us
    unnamed x2, blocking collectives  77.8 us
    reduce_scatter x1, waiting for transfers between devices, body(): lax.psum_scatter(local_grads[2].astype(jnp.bfloat16), 'dp', scatter_dimen...  67.7 us
    dot_general x10, matrix products, product(): return jnp.dot(left_mat, right_mat, preferred_element_type=jnp.float32)  65.3 us
    reduce_scatter x1, waiting for transfers between devices, body(): lax.psum_scatter(local_grads[3].astype(jnp.bfloat16), 'dp', scatter_dimen...  59.9 us
    all_gather x1, waiting for transfers between devices, body(): lax.all_gather(w_down, 'dp', axis=0, tiled=True)  40.1 us
    psum x1, blocking collectives, body(): lax.psum((jnp.sum(grad_roi, 0), jnp.sum(grad_roi * standard, 0)), ('dp',...  39.2 us
  transfers between devices with their start and end apart: 22, of which 8 were waited for; matrix products, arithmetic and copies ran while one was open for 26% of the time, Pallas kernels for 0%

commit v1 on v0

v1 whole, which is shorter than its diff:
```python
import functools

import jax
import jax.numpy as jnp
from jax import lax
from jax.experimental import pallas as pl
from jax.experimental.pallas import tpu as pltpu
from jax.sharding import PartitionSpec as P

HEADS = 12
FINE = 16
COARSE = 8
PAIR = 128
BOTH = ("dp", "mod")


def swapped(block, axis, distance):
    count = lax.axis_size(axis)
    route = []
    for low in range(count):
        high = low | 1 << distance
        if high != low and high < count:
            route += [(low, high), (high, low)]
    return lax.ppermute(block, axis, route)


def product(left_mat, right_mat):
    return jnp.dot(left_mat, right_mat, preferred_element_type=jnp.float32)


def inner_rows(left_mat, right_mat):
    return lax.dot_general(
        left_mat, right_mat, (((0,), (0,)), ((), ())), preferred_element_type=jnp.float32
    )


def outer_cols(left_mat, right_mat):
    return lax.dot_general(
        left_mat, right_mat, (((1,), (1,)), ((), ())), preferred_element_type=jnp.float32
    )


def norm_forward(hidden_in, gain_vec, bias_vec):
    average = jnp.mean(hidden_in, axis=-1, keepdims=True)
    centered = hidden_in - average
    variance = jnp.mean(centered * centered, axis=-1, keepdims=True)
    inverse = lax.rsqrt(variance + 1e-05)
    return centered * inverse * gain_vec + bias_vec, average, inverse


def norm_backward(grad_out, hidden_in, average, inverse, gain_vec):
    standard = (hidden_in - average) * inverse
    grad_gain = jnp.sum(grad_out * standard, 0)
    grad_bias = jnp.sum(grad_out, 0)
    scaled = grad_out * gain_vec
    mean_scaled = jnp.mean(scaled, axis=-1, keepdims=True)
    mean_cross = jnp.mean(scaled * standard, axis=-1, keepdims=True)
    grad_hidden = inverse * (scaled - mean_scaled - standard * mean_cross)
    return grad_hidden, grad_gain, grad_bias


def box_masks(boxes):
    left_edge = boxes[..., 0:1]
    top_edge = boxes[..., 1:2]
    right_edge = boxes[..., 2:3]
    bottom_edge = boxes[..., 3:4]
    fine_cell = jnp.arange(FINE * FINE, dtype=jnp.int32)
    fine_row = fine_cell // FINE
    fine_col = fine_cell % FINE
    inside_fine = (
        (fine_col >= left_edge)
        & (fine_col < right_edge)
        & (fine_row >= top_edge)
        & (fine_row < bottom_edge)
    )
    coarse_cell = jnp.arange(COARSE * COARSE, dtype=jnp.int32)
    coarse_row = coarse_cell // COARSE
    coarse_col = coarse_cell % COARSE
    inside_coarse = (
        (coarse_col >= left_edge // 2)
        & (coarse_col < (right_edge + 1) // 2)
        & (coarse_row >= top_edge // 2)
        & (coarse_row < (bottom_edge + 1) // 2)
    )
    coarse_area = jnp.sum(inside_coarse.astype(jnp.float32), -1, keepdims=True)
    fine_area = jnp.sum(inside_fine.astype(jnp.float32), -1, keepdims=True)
    return inside_coarse, inside_fine, coarse_area, fine_area


def key_live(counts_ref, page, text_slots, slots):
    col = lax.broadcasted_iota(jnp.int32, (1, slots), 1)
    text_count = counts_ref[page, 0]
    roi_count = counts_ref[page, 1]
    return (col < text_count) | ((col >= text_slots) & (col < text_slots + roi_count))


def attend_kernel(text_slots, scale, counts_ref, query_ref, key_ref, value_ref, out_ref, log_ref):
    slots = query_ref.shape[0]
    live = key_live(counts_ref, pl.program_id(0), text_slots, slots)
    lane = lax.broadcasted_iota(jnp.int32, (1, PAIR), 1)
    query = query_ref[...] * scale
    keys = key_ref[...]
    values = value_ref[...]
    parts = []
    logs = []
    for head in range(2):
        mine = (lane // (PAIR // 2)) == head
        masked = jnp.where(mine, query, jnp.zeros_like(query))
        scores = jnp.where(live, outer_cols(masked, keys), -1e30)
        highest = jnp.max(scores, -1, keepdims=True)
        exponent = jnp.exp(scores - highest)
        total = jnp.sum(exponent, -1, keepdims=True)
        weights = (exponent * (1.0 / total)).astype(jnp.bfloat16)
        parts.append(product(weights, values))
        logs.append(highest + jnp.log(total))
    first = lane < PAIR // 2
    out_ref[...] = jnp.where(first, parts[0], parts[1]).astype(jnp.bfloat16)
    log_ref[...] = jnp.where(first, logs[0], logs[1])


def attend_back_kernel(
    text_slots,
    scale,
    counts_ref,
    query_ref,
    key_ref,
    value_ref,
    grad_ref,
    log_ref,
    grad_query_ref,
    grad_key_ref,
    grad_value_ref,
):
    slots = query_ref.shape[0]
    live = key_live(counts_ref, pl.program_id(0), text_slots, slots)
    lane = lax.broadcasted_iota(jnp.int32, (1, PAIR), 1)
    query = query_ref[...] * scale
    keys = key_ref[...]
    values = value_ref[...]
    grad = grad_ref[...]
    logs = log_ref[...]
    queries_out = []
    keys_out = []
    values_out = []
    for head in range(2):
        mine = (lane // (PAIR // 2)) == head
        masked = jnp.where(mine, query, jnp.zeros_like(query))
        grad_mine = jnp.where(mine, grad, jnp.zeros_like(grad))
        log_col = logs[:, head * (PAIR // 2) : head * (PAIR // 2) + 1]
        weights = jnp.exp(jnp.where(live, outer_cols(masked, keys), -1e30) - log_col)
        grad_weights = outer_cols(grad_mine, values)
        delta = jnp.sum(grad_weights * weights, -1, keepdims=True)
        grad_scores = (weights * (grad_weights - delta)).astype(jnp.bfloat16)
        values_out.append(inner_rows(weights.astype(jnp.bfloat16), grad))
        queries_out.append(product(grad_scores, keys))
        keys_out.append(inner_rows(grad_scores, query))
    first = lane < PAIR // 2
    grad_query_ref[...] = (jnp.where(first, queries_out[0], queries_out[1]) * scale).astype(
        jnp.bfloat16
    )
    grad_key_ref[...] = jnp.where(first, keys_out[0], keys_out[1]).astype(jnp.bfloat16)
    grad_value_ref[...] = jnp.where(first, values_out[0], values_out[1]).astype(jnp.bfloat16)


def attention_call(kernel, counts, operands, out_types, page_count, flops):
    rows, width = operands[0].shape
    slots = rows // page_count
    spec = pl.BlockSpec((slots, PAIR), lambda page, pair, counts_ref: (page, pair))
    return pl.pallas_call(
        kernel,
        out_shape=tuple(jax.ShapeDtypeStruct((rows, width), kind) for kind in out_types),
        grid_spec=pltpu.PrefetchScalarGridSpec(
            num_scalar_prefetch=1,
            grid=(page_count, width // PAIR),
            in_specs=[spec] * len(operands),
            out_specs=tuple([spec] * len(out_types)),
        ),
        cost_estimate=pl.CostEstimate(
            flops=flops,
            bytes_accessed=rows * width * 2 * (len(operands) + len(out_types)),
            transcendentals=rows * slots * HEADS,
        ),
        compiler_params=pltpu.CompilerParams(
            dimension_semantics=("arbitrary", "arbitrary"), vmem_limit_bytes=40 << 20
        ),
    )(counts, *operands)


def gather_all(shard):
    mod_size = lax.axis_size("mod")
    piece = shard.shape[0] // mod_size
    mine = lax.dynamic_slice_in_dim(shard, lax.axis_index("mod") * piece, piece, 0)
    full = lax.all_gather(mine, BOTH, axis=0, tiled=True)
    return full.reshape(-1, *shard.shape)


def scatter_sum(stacked):
    dp_size, rows, width = stacked.shape
    part = lax.psum_scatter(
        stacked.reshape(dp_size * rows, width), BOTH, scatter_dimension=0, tiled=True
    )
    return lax.all_gather(part, "mod", axis=0, tiled=True)


def total_sum(stats):
    return lax.psum(stats, BOTH)


def body(
    text_emb,
    feature_maps,
    boxes,
    row_counts,
    w_roi,
    bn_gain,
    bn_bias,
    w_query,
    w_key,
    w_value,
    b_query,
    b_value,
    w_out,
    b_out,
    ln1_gain,
    ln1_bias,
    w_up,
    b_up,
    w_down,
    b_down,
    ln2_gain,
    ln2_bias,
    out_grad_text,
    out_grad_roi,
):
    page_count, text_slots, width = text_emb.shape
    roi_slots = boxes.shape[1]
    slots = text_slots + roi_slots
    channels = feature_maps.shape[2]
    head_size = width // HEADS
    scale = head_size ** (-0.5)
    coarse_cells = COARSE * COARSE
    rows = page_count * slots
    dp_size = lax.axis_size("dp")
    mod_size = lax.axis_size("mod")
    top_bit = mod_size.bit_length() - 2
    my_mod = lax.axis_index("mod")
    bf16 = jnp.bfloat16
    f32 = jnp.float32

    vectors = (
        bn_gain,
        bn_bias,
        b_query,
        b_value,
        b_out,
        ln1_gain,
        ln1_bias,
        b_down,
        ln2_gain,
        ln2_bias,
        b_up,
    )
    vector_len = sum(vector.shape[0] for vector in vectors)
    matrix_rows = w_roi.shape[0] + 4 * w_query.shape[0]
    quantum = 16 * mod_size
    vector_rows = -(-(matrix_rows + -(-vector_len // width)) // quantum) * quantum - matrix_rows
    packed_vectors = jnp.pad(
        jnp.concatenate(vectors), (0, vector_rows * width - vector_len)
    ).reshape(vector_rows, width)
    pieces = (w_roi, w_query, w_key, w_value, w_out, packed_vectors)
    first_full = gather_all(jnp.concatenate(pieces, 0))
    ff_parts = w_up.shape[1] // width
    up_blocks = w_up.reshape(w_up.shape[0], ff_parts, width).transpose(1, 0, 2)
    second_full = gather_all(
        jnp.concatenate([up_blocks.reshape(-1, width), w_down], 0)
    )

    far_maps, far_boxes, far_grad = swapped(
        (feature_maps, boxes, out_grad_roi), "mod", top_bit
    )
    counts = lax.dynamic_slice_in_dim(row_counts, my_mod * page_count, page_count, 0)
    text_live = jnp.arange(text_slots, dtype=jnp.int32)[None, :] < counts[:, 0:1]
    roi_live = jnp.arange(roi_slots, dtype=jnp.int32)[None, :] < counts[:, 1:2]
    live = jnp.concatenate([text_live, roi_live], 1).reshape(rows, 1).astype(f32)
    roi_mask = roi_live.reshape(-1, 1).astype(f32)

    def pooled_part(mask, maps, area):
        return (
            jnp.einsum("prc,pcf->prf", mask.astype(bf16), maps, preferred_element_type=f32) / area
        )

    coarse_in, fine_in, coarse_area, fine_area = box_masks(far_boxes)
    pooled = (
        jnp.concatenate(
            [
                pooled_part(coarse_in, far_maps[:, :coarse_cells], coarse_area),
                pooled_part(fine_in, far_maps[:, coarse_cells:], fine_area),
            ],
            -1,
        )
        .astype(bf16)
        .reshape(page_count * roi_slots, 2 * channels)
    )

    starts = []
    at = 0
    for piece in pieces:
        starts.append(at)
        at += piece.shape[0]

    def unpack(full, start, count):
        return full[:, start : start + count].reshape(dp_size * count, width)

    roi_weight, query_weight, key_weight, value_weight, out_weight = (
        unpack(first_full, start, piece.shape[0]) for start, piece in zip(starts[:5], pieces[:5])
    )
    flat_vectors = first_full[:, starts[5] :].reshape(dp_size, vector_rows * width)
    full_vectors = []
    at = 0
    for vector in vectors:
        full_vectors.append(
            flat_vectors[:, at : at + vector.shape[0]].reshape(-1).astype(f32)
        )
        at += vector.shape[0]
    (
        norm_gain,
        norm_bias,
        query_bias,
        value_bias,
        out_bias,
        first_gain,
        first_bias,
        down_bias,
        second_gain,
        second_bias,
        up_bias,
    ) = full_vectors
    up_rows = w_up.shape[0] * ff_parts
    up_weight = (
        second_full[:, :up_rows]
        .reshape(dp_size, ff_parts, w_up.shape[0], width)
        .transpose(0, 2, 1, 3)
        .reshape(width, ff_parts * width)
    )
    down_weight = unpack(second_full, up_rows, w_down.shape[0])

    projected = product(pooled, roi_weight)
    stats = jnp.stack(
        [
            jnp.sum(projected * roi_mask, 0),
            jnp.sum(projected * projected * roi_mask, 0),
            jnp.broadcast_to(jnp.sum(roi_mask), (width,)),
        ]
    )
    stats = total_sum(stats)
    number = stats[2:3]
    average = stats[0:1] / number
    variance = stats[1:2] / number - average * average
    inv_std = lax.rsqrt(variance + 1e-05)
    standard = (projected - average) * inv_std
    roi_rows = (standard * norm_gain + norm_bias).astype(bf16)
    rows_in = jnp.concatenate(
        [text_emb, roi_rows.reshape(page_count, roi_slots, width)], 1
    ).reshape(rows, width)
    queries = (product(rows_in, query_weight) + query_bias).astype(bf16)
    keys = product(rows_in, key_weight).astype(bf16)
    values = (product(rows_in, value_weight) + value_bias).astype(bf16)
    attention_flops = 4 * rows * slots * width
    context, logs = attention_call(
        functools.partial(attend_kernel, text_slots, scale),
        counts,
        (queries, keys, values),
        (bf16, f32),
        page_count,
        attention_flops,
    )
    first_in = rows_in.astype(f32) + product(context, out_weight) + out_bias
    normed, first_average, first_inverse = norm_forward(first_in, first_gain, first_bias)
    normed_low = normed.astype(bf16)
    hidden = product(normed_low, up_weight) + up_bias
    cumulative = 0.5 * (1.0 + lax.erf(hidden * (0.5**0.5)))
    activated = (hidden * cumulative).astype(bf16)
    slope = (
        cumulative + hidden * (jnp.exp(-0.5 * hidden * hidden) * 0.3989422804014327)
    ).astype(bf16)
    second_in = normed + product(activated, down_weight) + down_bias
    normed_out, second_average, second_inverse = norm_forward(
        second_in, second_gain, second_bias
    )
    output = (normed_out * live).astype(bf16).reshape(page_count, slots, width)
    out_text = output[:, :text_slots]
    out_roi = swapped(output[:, text_slots:], "mod", top_bit)

    upstream = (
        jnp.concatenate([out_grad_text, far_grad], 1).reshape(rows, width).astype(f32) * live
    )
    grad_second, grad_ln2_gain, grad_ln2_bias = norm_backward(
        upstream, second_in, second_average, second_inverse, second_gain
    )
    grad_mixed = grad_second.astype(bf16)
    grad_w_down = inner_rows(activated, grad_mixed).astype(bf16)
    grad_b_down = jnp.sum(grad_mixed.astype(f32), 0)
    grad_hidden = (outer_cols(grad_mixed, down_weight) * slope.astype(f32)).astype(bf16)
    grad_w_up = inner_rows(normed_low, grad_hidden).astype(bf16)
    grad_b_up = jnp.sum(grad_hidden.astype(f32), 0)
    up_stack = (
        grad_w_up.reshape(dp_size, w_up.shape[0], ff_parts, width)
        .transpose(0, 2, 1, 3)
        .reshape(dp_size, up_rows, width)
    )
    second_share = scatter_sum(
        jnp.concatenate([up_stack, grad_w_down.reshape(dp_size, -1, width)], 1)
    )
    grad_first, grad_ln1_gain, grad_ln1_bias = norm_backward(
        grad_second + outer_cols(grad_hidden, up_weight),
        first_in,
        first_average,
        first_inverse,
        first_gain,
    )
    grad_attended = grad_first.astype(bf16)
    grad_w_out = inner_rows(context, grad_attended).astype(bf16)
    grad_b_out = jnp.sum(grad_attended.astype(f32), 0)
    grad_context = outer_cols(grad_attended, out_weight).astype(bf16)
    grad_queries, grad_keys, grad_values = attention_call(
        functools.partial(attend_back_kernel, text_slots, scale),
        counts,
        (queries, keys, values, grad_context, logs),
        (bf16, bf16, bf16),
        page_count,
        attention_flops * 5 // 2,
    )
    grad_rows = (
        grad_first
        + outer_cols(grad_queries, query_weight)
        + outer_cols(grad_keys, key_weight)
        + outer_cols(grad_values, value_weight)
    ).reshape(page_count, slots, width)
    grad_text = grad_rows[:, :text_slots]
    grad_roi = grad_rows[:, text_slots:].reshape(page_count * roi_slots, width)
    sums = total_sum(jnp.stack([jnp.sum(grad_roi, 0), jnp.sum(grad_roi * standard, 0)]))
    grad_w_query = inner_rows(rows_in, grad_queries).astype(bf16)
    grad_b_query = jnp.sum(grad_queries.astype(f32), 0)
    grad_w_key = inner_rows(rows_in, grad_keys).astype(bf16)
    grad_w_value = inner_rows(rows_in, grad_values).astype(bf16)
    grad_b_value = jnp.sum(grad_values.astype(f32), 0)
    sum_grad = sums[0:1]
    sum_scaled = sums[1:2]
    grad_projected = (
        inv_std
        * (
            grad_roi * norm_gain
            - roi_mask * norm_gain * (sum_grad + standard * sum_scaled) / number
        )
    ).astype(bf16)
    grad_w_roi = inner_rows(pooled, grad_projected).astype(bf16)
    grad_pooled = (
        outer_cols(grad_projected, roi_weight)
        .astype(bf16)
        .reshape(page_count, roi_slots, 2 * channels)
    )
    own_pooled = swapped(grad_pooled, "mod", top_bit)
    own_coarse, own_fine, own_coarse_area, own_fine_area = box_masks(boxes)

    def spread(mask, grad, area):
        return jnp.einsum(
            "prc,prf->pcf",
            mask.astype(bf16),
            (grad.astype(f32) / area).astype(bf16),
            preferred_element_type=f32,
        )

    grad_maps = jnp.concatenate(
        [
            spread(own_coarse, own_pooled[..., :channels], own_coarse_area),
            spread(own_fine, own_pooled[..., channels:], own_fine_area),
        ],
        1,
    )

    grad_vectors = (
        jnp.zeros_like(grad_b_out),
        jnp.zeros_like(grad_b_out),
        grad_b_query,
        grad_b_value,
        grad_b_out,
        grad_ln1_gain,
        grad_ln1_bias,
        grad_b_down,
        grad_ln2_gain,
        grad_ln2_bias,
        grad_b_up,
    )
    vector_stack = jnp.concatenate(
        [vector.astype(bf16).reshape(dp_size, -1) for vector in grad_vectors], 1
    )
    vector_stack = jnp.pad(
        vector_stack, ((0, 0), (0, vector_rows * width - vector_len))
    ).reshape(dp_size, vector_rows, width)
    first_share = scatter_sum(
        jnp.concatenate(
            [
                grad.reshape(dp_size, -1, width)
                for grad in (grad_w_roi, grad_w_query, grad_w_key, grad_w_value, grad_w_out)
            ]
            + [vector_stack],
            1,
        )
    ).astype(f32)
    own_w_roi, own_w_query, own_w_key, own_w_value, own_w_out = (
        first_share[start : start + piece.shape[0]]
        for start, piece in zip(starts[:5], pieces[:5])
    )
    flat_share = first_share[starts[5] :].reshape(-1)
    vector_shares = []
    at = 0
    for vector in vectors:
        vector_shares.append(flat_share[at : at + vector.shape[0]])
        at += vector.shape[0]
    own_w_up = (
        second_share[:up_rows]
        .reshape(ff_parts, w_up.shape[0], width)
        .transpose(1, 0, 2)
        .reshape(w_up.shape)
        .astype(f32)
    )
    own_w_down = second_share[up_rows:].astype(f32)
    share_len = width // dp_size
    share_start = lax.axis_index("dp") * share_len
    gain_share = lax.dynamic_slice_in_dim(sums[1], share_start, share_len, 0)
    bias_share = lax.dynamic_slice_in_dim(sums[0], share_start, share_len, 0)
    return (
        out_text,
        out_roi,
        grad_text,
        grad_maps,
        own_w_roi,
        gain_share,
        bias_share,
        own_w_query,
        own_w_key,
        own_w_value,
        vector_shares[2],
        vector_shares[3],
        own_w_out,
        vector_shares[4],
        vector_shares[5],
        vector_shares[6],
        own_w_up,
        vector_shares[10],
        own_w_down,
        vector_shares[7],
        vector_shares[8],
        vector_shares[9],
    )


def solution(mesh):
    in_specs = (
        P(("dp", "mod"), None, None),
        P(("dp", "mod"), None, None),
        P(("dp", "mod"), None, None),
        P("dp", None),
        P("dp", None),
        P("dp"),
        P("dp"),
        P("dp", None),
        P("dp", None),
        P("dp", None),
        P("dp"),
        P("dp"),
        P("dp", None),
        P("dp"),
        P("dp"),
        P("dp"),
        P("dp", None),
        P("dp"),
        P("dp", None),
        P("dp"),
        P("dp"),
        P("dp"),
        P(("dp", "mod"), None, None),
        P(("dp", "mod"), None, None),
    )
    out_specs = (
        P(("dp", "mod"), None, None),
        P(("dp", "mod"), None, None),
        P(("dp", "mod"), None, None),
        P(("dp", "mod"), None, None),
        P("dp", None),
        P("dp"),
        P("dp"),
        P("dp", None),
        P("dp", None),
        P("dp", None),
        P("dp"),
        P("dp"),
        P("dp", None),
        P("dp"),
        P("dp"),
        P("dp"),
        P("dp", None),
        P("dp"),
        P("dp", None),
        P("dp"),
        P("dp"),
        P("dp"),
    )
    return jax.shard_map(body, mesh=mesh, in_specs=in_specs, out_specs=out_specs, check_vma=False)
```

time: 1050 us -> 556 us (0.53)
  waiting for transfers between devices: 399 us -> 196 us
  blocking collectives: 221 us -> 91.2 us
  matrix products: 207 us -> 78.1 us
  Pallas kernels: 0 us -> 44.4 us
  other arithmetic: 71.5 us -> 28.4 us
  local copies, waits for them, and re-layouts: 120 us -> 85.6 us
    reduce_scatter x7 -> x2, waiting for transfers between devices: 325 us -> 129 us  [scatter_sum(): lax.psum_scatter(stacked.reshape(dp_size * rows, width), BOTH, scatter_di...]
    unnamed x2 -> x0, blocking collectives: 77.8 us -> none
    dot_general x16 -> x4, matrix products: 65.3 us -> 3.03 us  [the longest x2 2.37 us: spread(): jnp.einsum('prc,prf->pcf', mask.astype(bf16), (grad.astype(f32) / area).a...]
    all_gather x2 -> x1, blocking collectives: 58.8 us -> 8.71 us  [scatter_sum(): return lax.all_gather(part, 'mod', axis=0, tiled=True)]
    pallas_call x0 -> x2, Pallas kernels: none -> 44.4 us  [attention_call(): pl.pallas_call(kernel, out_shape=tuple((jax.ShapeDtypeStruct((rows, width...]
    dot_general x10 -> x7, matrix products: 65.3 us -> 21.2 us  [product(): return jnp.dot(left_mat, right_mat, preferred_element_type=jnp.float32)]
    convert_element_type x31 -> x5, other arithmetic: 35.9 us -> 3.36 us  [the longest x1 2.38 us: body(): own_w_down = second_share[up_rows:].astype(f32)]
    psum x1 -> x0, waiting for transfers between devices: 21.5 us -> none  [body(): lax.psum(shares[0].astype(jnp.bfloat16), 'mod').astype(jnp.float32)]
  transfers between devices with their start and end apart: 22 -> 10, of which waited for: 8 -> 5; matrix products, arithmetic and copies ran while one was open for 26% -> 15% of each run, Pallas kernels for 0% -> 8%
where the time goes in v1:
time: 556 us; the launch traced here: 547 us
  waiting for transfers between devices  196 us (35%)
  blocking collectives  91.2 us (16%)
  local copies, waits for them, and re-layouts  85.6 us (15%)
  matrix products  78.1 us (14%)
  Pallas kernels  44.4 us (8%)
  other arithmetic  28.4 us (5%)
  between operations  15.7 us (3%)
  starting transfers between devices  7.29 us (1%)
    reduce_scatter x2, waiting for transfers between devices, scatter_sum(): lax.psum_scatter(stacked.reshape(dp_size * rows, width), BOTH, scatter_di...  129 us
    psum x2, blocking collectives, total_sum(): return lax.psum(stats, BOTH)  82.5 us
    all_gather x2, waiting for transfers between devices, gather_all(): full = lax.all_gather(mine, BOTH, axis=0, tiled=True)  55.3 us
    pallas_call x2, Pallas kernels, attention_call(): pl.pallas_call(kernel, out_shape=tuple((jax.ShapeDtypeStruct((rows, width...  44.4 us
    dot_general x7, matrix products, outer_cols(): lax.dot_general(left_mat, right_mat, (((1,), (1,)), ((), ())), preferred_...  31.5 us
    unnamed x209, local copies, waits for them, and re-layouts  28.6 us
    dot_general x7, matrix products, inner_rows(): lax.dot_general(left_mat, right_mat, (((0,), (0,)), ((), ())), preferred_...  22.4 us
    dot_general x7, matrix products, product(): return jnp.dot(left_mat, right_mat, preferred_element_type=jnp.float32)  21.2 us
  transfers between devices with their start and end apart: 10, of which 5 were waited for; matrix products, arithmetic and copies ran while one was open for 15% of the time, Pallas kernels for 8%

profile of v1, /device:TPU:0, one launch (start us, length us, event | category | flops | bytes accessed | tf_op | source)
XLA Modules:
  0.0 547.1 jit_solution(14364133216075286562)
XLA Ops:
  8.3 7.4 %concatenate.45 = bf16[1344]{0:T(1024)(128)(2,1)S(1)} concatenate(bf16[96]{0:T(256)(128)(2,1)} %param.29, bf16[96]{0:T(256)(128)(2,1)} %param.30, bf16[96]{0:T(256)(128)(2,1)} %param.34, bf16[96]{0:T(256)(128)(2,1)} %param.35, bf16[96]{0:T(256)(128)(2,1)} %param.37, bf16[96]{0:T(256)(128)(2,1)} %param.38, bf16[96]{0:T(256)(128)(2,1)} %param.39, bf16[96]{0:T(256)(128)(2,1)} %param.43, ...), dimensions={0} | concatenate | bytes 5376 | tf_op jit(solution)/shard_map/concatenate | solution.py:268
  31.8 5.7 %collective-permute-done.1 = bf16[2,320,256]{2,1,0:T(8,128)(2,1)S(1)} collective-permute-done((bf16[2,320,256]{2,1,0:T(8,128)(2,1)S(1)}, bf16[2,320,256]{2,1,0:T(8,128)(2,1)S(1)}, u32[]{:S(2)}, u32[]{:S(2)}) %collective-permute-start.1) | collective-permute-done | bytes 327712 | tf_op jit(solution)/shard_map/ppermute | solution.py:24
  38.2 55.3 %all-gather.4.cloned.1.call-done = bf16[4096,768]{1,0:T(8,128)(2,1)} async-done(((bf16[128,768]{1,0:T(8,128)(2,1)}), bf16[4096,768]{1,0:T(8,128)(2,1)}) %all-gather.4.cloned.1.call-update) | async-done | bytes 6291472 | tf_op jit(solution)/shard_map/all_gather | solution.py:193
  105.3 40.1 %psum.14 = f32[3,768]{1,0:T(4,128)S(1)} all-reduce(f32[3,768]{1,0:T(4,128)S(1)} %maximum_maximum_fusion), channel_id=1, replica_groups=mesh['dp'=8,'mod'=4] {'dp','mod'}, use_global_device_ids=true, to_apply=%region_5.6 | all-reduce | flops 2304 | bytes 18432 | tf_op jit(solution)/shard_map/psum | solution.py:206
  147.5 3.3 fusion.37
  155.2 18.6 %shard_map.399 = (bf16[1024,768]{1,0:T(8,128)(2,1)S(1)}, f32[1024,768]{1,0:T(8,128)S(1)}) custom-call(s32[2,2]{1,0:T(2,128)S(1)} %copy.62.counts_ref, bf16[1024,768]{1,0:T(8,128)(2,1)S(1)} %add_convert_fusion.1.query_ref, bf16[1024,768]{1,0:T(8,128)(2,1)S(1)} %convolution_convert_fusion.3.key_ref, bf16[1024,768]{1,0:T(8,128)(2,1)S(1)} %add_convert_fusion.value_ref), custom_call_target="tpu_custom_call" | custom-call | flops 1610612736 | bytes 7864320 | tf_op jit(solution)/shard_map/pallas_call | solution.py:169
  177.7 6.7 %fusion.36 = (bf16[8,384,768]{2,1,0:T(8,128)(2,1)}, bf16[8,384,768]{2,1,0:T(8,128)(2,1)S(1)}) fusion(bf16[8,768,768]{2,1,0:T(8,128)(2,1)} %bitcast.142), kind=kLoop, calls=%fused_computation.194 | loop fusion | bytes 18874368 | tf_op jit(solution)/shard_map/slice | solution.py:312
  184.4 3.6 copy.58
  189.2 9.6 %multiply_convert_fusion.1 = (bf16[1024,3072]{1,0:T(8,128)(2,1)S(1)}, f32[1024,3072]{1,0:T(8,128)}) fusion(f32[3072]{0:T(1024)S(1)} %copy-done.55, bf16[768,3072]{1,0:T(8,128)(2,1)S(1)} %bitcast.147, f32[1024,768]{1,0:T(8,128)S(1)} %get-tuple-element.118, f32[768]{0:T(1024)S(1)} %copy-done.73, f32[768]{0:T(1024)S(1)} %copy-done.49, f32[1024]{0:T(1024)S(1)} %copy-done.51, ...), kind=kOutput, calls=%fused_computation.7 | convolution fusion | flops 4854644736 | bytes 26765312 | tf_op jit(solution)/shard_map/dot_general | solution.py:28
  198.9 5.5 fusion.42
  205.6 3.3 multiply_reduce_fusion
  210.9 7.1 %convolution_convert_fusion = bf16[3072,768]{1,0:T(8,128)(2,1)} fusion(bf16[1024,3072]{1,0:T(8,128)(2,1)S(1)} %get-tuple-element.119, f32[1024,768]{1,0:T(8,128)S(1)} %get-tuple-element.54), kind=kOutput, calls=%fused_computation.10 | convolution fusion | flops 4834983936 | bytes 14155776 | tf_op jit(solution)/shard_map/dot_general | solution.py:32
  218.0 11.7 %fusion.43 = (bf16[3072]{0:T(1024)(128)(2,1)S(1)}, bf16[1024,3072]{1,0:T(8,128)(2,1)S(1)}) fusion(f32[1024,3072]{1,0:T(8,128)} %get-tuple-element.120, f32[3072]{0:T(1024)S(1)} %copy-done.55, bf16[3072,768]{1,0:T(8,128)(2,1)S(1)} %bitcast.152, f32[1024,768]{1,0:T(8,128)S(1)} %get-tuple-element.54), kind=kOutput, calls=%fused_computation.201 | convolution fusion | flops 4876661760 | bytes 26757120 | tf_op jit(solution)/shard_map/dot_general | solution.py:38
  232.3 8.0 %convolution_convert_fusion.1 = bf16[768,3072]{1,0:T(8,128)(2,1)} fusion(bf16[1024,3072]{1,0:T(8,128)(2,1)S(1)} %get-tuple-element.125, f32[1024,768]{1,0:T(8,128)S(1)} %get-tuple-element.118, f32[768]{0:T(1024)S(1)} %copy-done.73, f32[768]{0:T(1024)S(1)} %copy-done.49, f32[1024]{0:T(1024)S(1)} %copy-done.51, f32[1024]{0:T(1024)S(1)} %copy-done.44), kind=kOutput, calls=%fused_computation.11 | convolution fusion | flops 4838129664 | bytes 14170112 | tf_op jit(solution)/shard_map/dot_general | solution.py:32
  240.4 9.7 %reshape.441 = bf16[8,96,4,768]{3,2,1,0:T(4,128)(2,1)} reshape(bf16[768,3072]{1,0:T(8,128)(2,1)} %convolution_convert_fusion.1) | data formatting | bytes 9437184 | tf_op jit(solution)/shard_map/reshape | solution.py:407
  250.1 3.2 copy.59
  253.3 6.6 %pad_maximum_fusion = bf16[8,768,768]{2,1,0:T(8,128)(2,1)} fusion(bf16[8,384,768]{2,1,0:T(8,128)(2,1)} %bitcast.153, bf16[8,384,768]{2,1,0:T(8,128)(2,1)S(1)} %bitcast.139), kind=kLoop, calls=%fused_computation.9 | loop fusion | flops 18874368 | bytes 18874368 | tf_op jit(solution)/shard_map/concatenate | solution.py:412
  260.6 10.3 %multiply_reduce_fusion.1 = (bf16[768]{0:T(1024)(128)(2,1)S(1)}, f32[1024]{0:T(1024)S(1)}, f32[1024]{0:T(1024)S(1)}, bf16[768]{0:T(1024)(128)(2,1)S(1)}, f32[1024,768]{1,0:T(8,128)S(1)}) fusion(f32[1024,768]{1,0:T(8,128)S(1)} %get-tuple-element.118, f32[1024]{0:T(1024)S(1)} %copy-done.52, f32[1024]{0:T(1024)S(1)} %copy-done.45, f32[768]{0:T(1024)S(1)} %copy-done.50, ...), kind=kOutput, calls=%fused_computation.14 | convolution fusion | flops 4839698432 | bytes 20469760 | tf_op jit(solution)/shard_map/dot_general | solution.py:38
  276.5 25.9 %shard_map.400 = (bf16[1024,768]{1,0:T(8,128)(2,1)S(1)}, bf16[1024,768]{1,0:T(8,128)(2,1)S(1)}, bf16[1024,768]{1,0:T(8,128)(2,1)S(1)}) custom-call(s32[2,2]{1,0:T(2,128)S(1)} %copy.62.counts_ref, bf16[1024,768]{1,0:T(8,128)(2,1)S(1)} %copy-done.14, bf16[1024,768]{1,0:T(8,128)(2,1)S(1)} %copy-done.10, bf16[1024,768]{1,0:T(8,128)(2,1)S(1)} %copy-done.12, ...), custom_call_target="tpu_custom_call" | custom-call | flops 4026531840 | bytes 12582912 | tf_op jit(solution)/shard_map/pallas_call | solution.py:169
  315.0 42.4 %psum.15 = f32[2,768]{1,0:T(2,128)S(1)} all-reduce(f32[2,768]{1,0:T(2,128)S(1)} %pad_maximum_fusion.7), channel_id=1, replica_groups=mesh['dp'=8,'mod'=4] {'dp','mod'}, use_global_device_ids=true, to_apply=%region_16.17 | all-reduce | flops 1536 | bytes 12288 | tf_op jit(solution)/shard_map/psum | solution.py:206
  380.0 18.7 %reduce-scatter.5.cloned.1.call-done = bf16[192,768]{1,0:T(8,128)(2,1)} async-done(((bf16[6144,768]{1,0:T(8,128)(2,1)}), bf16[192,768]{1,0:T(8,128)(2,1)}) %reduce-scatter.5.cloned.1.call-update) | async-done | bytes 294928 | tf_op jit(solution)/shard_map/reduce_scatter | solution.py:199
  407.5 110.4 %reduce-scatter.3.cloned.1.call-done = bf16[128,768]{1,0:T(8,128)(2,1)} async-done(((bf16[4096,768]{1,0:T(8,128)(2,1)}), bf16[128,768]{1,0:T(8,128)(2,1)}) %reduce-scatter.3.cloned.1.call-update) | async-done | bytes 196624 | tf_op jit(solution)/shard_map/reduce_scatter | solution.py:199
  517.9 8.7 %all_gather.14 = bf16[512,768]{1,0:T(8,128)(2,1)S(1)} all-gather(bf16[128,768]{1,0:T(8,128)(2,1)} %reduce-scatter.3.cloned.1.call-done), channel_id=1, replica_groups=mesh['dp'=8,'mod'=4] {'mod'}, dimensions={0}, use_global_device_ids=true | all-gather | bytes 983040 | tf_op jit(solution)/shard_map/all_gather | solution.py:202
  529.6 6.1 %all-gather.8.cloned.1.call-done = bf16[768,768]{1,0:T(8,128)(2,1)} async-done(((bf16[192,768]{1,0:T(8,128)(2,1)}), bf16[768,768]{1,0:T(8,128)(2,1)}) %all-gather.8.cloned.1.call-update) | async-done | bytes 1179664 | tf_op jit(solution)/shard_map/all_gather | solution.py:202
  (336 shorter events, 103.3 us)
Async XLA Ops:
  7.2 86.3 %all-gather.4.cloned.1.call-start = ((), (), s32[]{:S(2)}) async-start(), calls=%async_computation.2 | async-start | bytes 6488064 | tf_op jit(solution)/shard_map/all_gather | solution.py:193
  20.3 157.4 %all-gather.6.cloned.1.call-start = ((), (), s32[]{:S(2)}) async-start(), calls=%async_computation.3 | async-start | bytes 9732096 | tf_op jit(solution)/shard_map/all_gather | solution.py:193
  22.5 376.2 %reduce-scatter.5.cloned.1.call-start = ((), (), s32[]{:S(2)}) async-start(), calls=%async_computation.5 | async-start | bytes 9732096 | tf_op jit(solution)/shard_map/reduce_scatter | solution.py:199
  22.5 7.7 %collective-permute-start = (s32[2,128,4]{1,2,0:T(4,128)S(1)}, s32[2,128,4]{1,2,0:T(4,128)S(1)}, u32[]{:S(2)}, u32[]{:S(2)}) collective-permute-start(s32[2,128,4]{1,2,0:T(4,128)S(1)} %copy-done.60), channel_id=1, source_target_pairs={{0,2},{2,0},{1,3},{3,1},{4,6},{6,4},{5,7},{7,5},{8,10},{10,8},{9,1... | collective-permute-start | bytes 12296 | tf_op jit(solution)/shard_map/ppermute | solution.py:24
  25.6 12.0 %collective-permute-start.1 = (bf16[2,320,256]{2,1,0:T(8,128)(2,1)S(1)}, bf16[2,320,256]{2,1,0:T(8,128)(2,1)S(1)}, u32[]{:S(2)}, u32[]{:S(2)}) collective-permute-start(bf16[2,320,256]{2,1,0:T(8,128)(2,1)S(1)} %copy-done.92), channel_id=1, source_target_pairs={{0,2},{2,0},{1,3},{3,1},{4,6},{6,4},{5,7},{7,5},{8,10},{10,8},{9,1... | collective-permute-start | bytes 983048 | tf_op jit(solution)/shard_map/ppermute | solution.py:24
  25.6 77.7 %collective-permute-start.3 = (bf16[2,128,768]{2,1,0:T(8,128)(2,1)}, bf16[2,128,768]{2,1,0:T(8,128)(2,1)S(1)}, u32[]{:S(2)}, u32[]{:S(2)}) collective-permute-start(bf16[2,128,768]{2,1,0:T(8,128)(2,1)} %param.47), channel_id=1, source_target_pairs={{0,2},{2,0},{1,3},{3,1},{4,6},{6,4},{5,7},{7,5},{8,10},{10,8},{9,1... | collective-permute-start | bytes 1179656 | tf_op jit(solution)/shard_map/ppermute | solution.py:24
  27.8 67.8 %copy-start.69 = (s32[256]{0:T(256)}, s32[256]{0:T(256)S(1)}, u32[]{:S(2)}) copy-start(s32[256]{0:T(256)S(1)} %get-tuple-element.126) | copy-start | bytes 3076
  27.8 67.8 %copy-start.71 = (s32[256]{0:T(256)}, s32[256]{0:T(256)S(1)}, u32[]{:S(2)}) copy-start(s32[256]{0:T(256)S(1)} %get-tuple-element.127) | copy-start | bytes 3076
  28.0 67.6 %copy-start.59 = (f32[256]{0:T(256)}, f32[256]{0:T(256)S(1)}, u32[]{:S(2)}) copy-start(f32[256]{0:T(256)S(1)} %get-tuple-element.115) | copy-start | bytes 3076
  28.8 66.8 %copy-start.61 = (s32[2,128,1]{1,2,0:T(1,128)}, s32[2,128,1]{1,2,0:T(1,128)S(1)}, u32[]{:S(2)}) copy-start(s32[2,128,1]{1,2,0:T(1,128)S(1)} %get-tuple-element.108) | copy-start | bytes 3076
  28.8 66.8 %copy-start.63 = (s32[2,128,1]{1,2,0:T(1,128)}, s32[2,128,1]{1,2,0:T(1,128)S(1)}, u32[]{:S(2)}) copy-start(s32[2,128,1]{1,2,0:T(1,128)S(1)} %get-tuple-element.109) | copy-start | bytes 3076
  28.8 66.8 %copy-start.65 = (s32[2,128,1]{1,2,0:T(1,128)}, s32[2,128,1]{1,2,0:T(1,128)S(1)}, u32[]{:S(2)}) copy-start(s32[2,128,1]{1,2,0:T(1,128)S(1)} %get-tuple-element.110) | copy-start | bytes 3076
  28.8 66.8 %copy-start.67 = (s32[2,128,1]{1,2,0:T(1,128)}, s32[2,128,1]{1,2,0:T(1,128)S(1)}, u32[]{:S(2)}) copy-start(s32[2,128,1]{1,2,0:T(1,128)S(1)} %get-tuple-element.111) | copy-start | bytes 3076
  28.8 66.8 %copy-start.78 = (s32[2,128,1]{1,2,0:T(1,128)}, s32[2,128,1]{1,2,0:T(1,128)S(1)}, u32[]{:S(2)}) copy-start(s32[2,128,1]{1,2,0:T(1,128)S(1)} %get-tuple-element.104) | copy-start | bytes 3076
  28.9 66.8 %copy-start.80 = (s32[2,128,1]{1,2,0:T(1,128)}, s32[2,128,1]{1,2,0:T(1,128)S(1)}, u32[]{:S(2)}) copy-start(s32[2,128,1]{1,2,0:T(1,128)S(1)} %get-tuple-element.105) | copy-start | bytes 3076
  28.9 66.8 %copy-start.82 = (s32[2,128,1]{1,2,0:T(1,128)}, s32[2,128,1]{1,2,0:T(1,128)S(1)}, u32[]{:S(2)}) copy-start(s32[2,128,1]{1,2,0:T(1,128)S(1)} %get-tuple-element.106) | copy-start | bytes 3076
  28.9 66.8 %copy-start.84 = (s32[2,128,1]{1,2,0:T(1,128)}, s32[2,128,1]{1,2,0:T(1,128)S(1)}, u32[]{:S(2)}) copy-start(s32[2,128,1]{1,2,0:T(1,128)S(1)} %get-tuple-element.107) | copy-start | bytes 3076
  28.9 66.8 %copy-start.88 = (s32[64]{0:T(128)}, s32[64]{0:T(128)S(1)}, u32[]{:S(2)}) copy-start(s32[64]{0:T(128)S(1)} %get-tuple-element.128) | copy-start | bytes 772
  28.9 66.8 %copy-start.90 = (s32[64]{0:T(128)}, s32[64]{0:T(128)S(1)}, u32[]{:S(2)}) copy-start(s32[64]{0:T(128)S(1)} %get-tuple-element.129) | copy-start | bytes 772
  38.2 57.9 %copy-start.42 = (bf16[2,128,256]{2,1,0:T(8,128)(2,1)}, bf16[2,128,256]{2,1,0:T(8,128)(2,1)S(1)}, u32[]{:S(2)}) copy-start(bf16[2,128,256]{2,1,0:T(8,128)(2,1)S(1)} %fusion.8) | copy-start | bytes 393220
  259.9 257.9 %reduce-scatter.3.cloned.1.call-start = ((), (), s32[]{:S(2)}) async-start(), calls=%async_computation.4 | async-start | bytes 6488064 | tf_op jit(solution)/shard_map/reduce_scatter | solution.py:199
  373.7 162.0 %all-gather.8.cloned.1.call-start = ((), (), s32[]{:S(2)}) async-start(), calls=%async_computation.6 | async-start | bytes 1474560 | tf_op jit(solution)/shard_map/all_gather | solution.py:202
  376.2 28.0 %collective-permute-start.4 = (bf16[2,128,512]{2,1,0:T(8,128)(2,1)}, bf16[2,128,512]{2,1,0:T(8,128)(2,1)}, u32[]{:S(2)}, u32[]{:S(2)}) collective-permute-start(bf16[2,128,512]{2,1,0:T(8,128)(2,1)} %bitcast.33), channel_id=1, source_target_pairs={{0,2},{2,0},{1,3},{3,1},{4,6},{6,4},{5,7},{7,5},{8,10},{10,8},{9,1... | collective-permute-start | bytes 786440 | tf_op jit(solution)/shard_map/ppermute | solution.py:24
  379.9 27.6 %collective-permute-start.2 = (bf16[2,128,768]{2,1,0:T(8,128)(2,1)}, bf16[2,128,768]{2,1,0:T(8,128)(2,1)S(1)}, u32[]{:S(2)}, u32[]{:S(2)}) collective-permute-start(bf16[2,128,768]{2,1,0:T(8,128)(2,1)} %slice.267), channel_id=1, source_target_pairs={{0,2},{2,0},{1,3},{3,1},{4,6},{6,4},{5,7},{7,5},{8,10},{10,8},{9,1... | collective-permute-start | bytes 1179656 | tf_op jit(solution)/shard_map/ppermute | solution.py:24
  (82 other events, 602.7 us)
Sparse Core Ops, SparseCore 0:
  20.4 73.1 all-gather.3
  97.0 80.3 all-gather.5
  260.1 138.5 reduce-scatter.4
  404.2 113.6 reduce-scatter.2
  519.3 16.3 all-gather.7

commit v2 on v1

--- a/solution.py
+++ b/solution.py
@@ -202,8 +202,379 @@
     return lax.all_gather(part, "mod", axis=0, tiled=True)
 
 
-def total_sum(stats):
-    return lax.psum(stats, BOTH)
+MESH = pl.DeviceIdType.MESH
+
+
+def grid_sizes():
+    dp_size = lax.axis_size("dp")
+    mod_size = lax.axis_size("mod")
+    short = 1 << ((dp_size.bit_length() - 1) // 2)
+    return dp_size // short, short, mod_size // 2
+
+
+def place(sizes):
+    _, short, _ = sizes
+    dp_index = lax.axis_index("dp")
+    mod_index = lax.axis_index("mod")
+    return dp_index // short, dp_index % short, mod_index // 2, mod_index % 2
+
+
+def device_at(sizes, row, col, wide, core):
+    return {"dp": row * sizes[1] + col, "mod": wide * 2 + core}
+
+
+def greet(peers):
+    barrier = pltpu.get_barrier_semaphore()
+    for peer in peers:
+        pl.semaphore_signal(barrier, inc=1, device_id=peer, device_id_type=MESH)
+    pl.semaphore_wait(barrier, len(peers))
+
+
+def send(source, target, send_sem, recv_sem, peer):
+    copy = pltpu.make_async_remote_copy(
+        src_ref=source,
+        dst_ref=target,
+        send_sem=send_sem,
+        recv_sem=recv_sem,
+        device_id=peer,
+        device_id_type=MESH,
+    )
+    copy.start()
+    return copy
+
+
+def total_kernel(mod_size, dp_size, stats_ref, out_ref, near, far, send_sem, recv_sem):
+    my_mod = lax.axis_index("mod")
+    my_dp = lax.axis_index("dp")
+    near_peers = [{"mod": (my_mod + step) % mod_size} for step in range(1, mod_size)]
+    far_peers = [{"dp": (my_dp + step) % dp_size} for step in range(1, dp_size)]
+    greet(near_peers + far_peers)
+    near[my_mod] = stats_ref[...]
+    copies = [
+        send(stats_ref, near.at[my_mod], send_sem.at[at], recv_sem.at[at], peer)
+        for at, peer in enumerate(near_peers)
+    ]
+    for copy in copies:
+        copy.wait()
+    group = near[0]
+    for at in range(1, mod_size):
+        group = group + near[at]
+    far[my_dp] = group
+    copies = [
+        send(
+            far.at[my_dp],
+            far.at[my_dp],
+            send_sem.at[mod_size - 1 + at],
+            recv_sem.at[mod_size - 1 + at],
+            peer,
+        )
+        for at, peer in enumerate(far_peers)
+    ]
+    for copy in copies:
+        copy.wait()
+    total = far[0]
+    for at in range(1, dp_size):
+        total = total + far[at]
+    out_ref[...] = total
+
+
+def total_sum(stats, call_id):
+    mod_size = lax.axis_size("mod")
+    dp_size = lax.axis_size("dp")
+    messages = mod_size + dp_size - 2
+    padded = jnp.pad(stats, ((0, -stats.shape[0] % 8), (0, 0)))
+    vmem = pl.BlockSpec(memory_space=pltpu.VMEM)
+    return pl.pallas_call(
+        functools.partial(total_kernel, mod_size, dp_size),
+        out_shape=jax.ShapeDtypeStruct(padded.shape, jnp.float32),
+        in_specs=[vmem],
+        out_specs=vmem,
+        scratch_shapes=[
+            pltpu.VMEM((mod_size, *padded.shape), jnp.float32),
+            pltpu.VMEM((dp_size, *padded.shape), jnp.float32),
+            pltpu.SemaphoreType.DMA((messages,)),
+            pltpu.SemaphoreType.DMA((messages,)),
+        ],
+        compiler_params=pltpu.CompilerParams(
+            collective_id=call_id, has_side_effects=True, vmem_limit_bytes=8 << 20
+        ),
+        name=f"total_{call_id}",
+    )(padded)
+
+
+def gather_kernel(sizes, shard_ref, out_ref, send_sem, recv_sem, local_sem):
+    rows, cols, wides = sizes
+    row, col, wide, core = place(sizes)
+    row_peers = [((row + step) % rows, col, wide, core) for step in range(1, rows)]
+    col_peers = [(row, (col + step) % cols, wide, core) for step in range(1, cols)]
+    wide_peers = [(row, col, (wide + step) % wides, core) for step in range(1, wides)]
+    partner = (row, col, wide, 1 - core)
+    own = pltpu.make_async_copy(shard_ref, out_ref.at[row, col], local_sem)
+    own.start()
+    own.wait()
+    greet(
+        [device_at(sizes, *peer) for peer in row_peers + col_peers + wide_peers + [partner]]
+    )
+    used = [0]
+    pending = []
+
+    def push(source, target, peer):
+        at = used[0]
+        used[0] += 1
+        return send(
+            source, target, send_sem.at[at], recv_sem.at[at], device_at(sizes, *peer)
+        )
+
+    def arrive(copies):
+        for copy in copies:
+            copy.wait_recv()
+        pending.extend(copies)
+
+    split_rows = [
+        push(shard_ref.at[core, 0, wide], out_ref.at[row, col, core, 0, wide], peer)
+        for peer in row_peers
+    ]
+    whole_rows = [
+        push(shard_ref.at[core, 1], out_ref.at[row, col, core, 1], peer) for peer in row_peers
+    ]
+    arrive(split_rows)
+    view = out_ref.at[:, col, core, 0, wide]
+    split_cols = [push(view, view, peer) for peer in col_peers]
+    arrive(whole_rows)
+    view = out_ref.at[:, col, core, 1]
+    whole_cols = [push(view, view, peer) for peer in col_peers]
+    arrive(split_cols)
+    view = out_ref.at[:, :, core, 0, wide]
+    split_wide = [push(view, view, peer) for peer in wide_peers]
+    arrive(whole_cols)
+    view = out_ref.at[:, :, core, 1]
+    whole_core = [push(view, view, partner)]
+    arrive(split_wide)
+    view = out_ref.at[:, :, core, 0]
+    split_core = [push(view, view, partner)]
+    arrive(whole_core)
+    arrive(split_core)
+    for copy in pending:
+        copy.wait_send()
+
+
+def quick_gather(shard, call_id):
+    sizes = grid_sizes()
+    rows, cols, wides = sizes
+    height, width = shard.shape
+    part = height // (4 * wides)
+    messages = 2 * (rows - 1) + 2 * (cols - 1) + (wides - 1) + 2
+    vmem = pl.BlockSpec(memory_space=pltpu.VMEM)
+    out = pl.pallas_call(
+        functools.partial(gather_kernel, sizes),
+        out_shape=jax.ShapeDtypeStruct((rows, cols, 2, 2, wides, part, width), shard.dtype),
+        in_specs=[vmem],
+        out_specs=vmem,
+        scratch_shapes=[
+            pltpu.SemaphoreType.DMA((messages,)),
+            pltpu.SemaphoreType.DMA((messages,)),
+            pltpu.SemaphoreType.DMA(()),
+        ],
+        compiler_params=pltpu.CompilerParams(
+            collective_id=call_id, has_side_effects=True, vmem_limit_bytes=32 << 20
+        ),
+        name="gather_weights",
+    )(shard.reshape(2, 2, wides, part, width))
+    return out.reshape(rows * cols, height, width)
+
+
+def add_into(target, base, extras):
+    total = base.astype(jnp.float32)
+    for extra in extras:
+        total = total + extra.astype(jnp.float32)
+    target[...] = total.astype(target.dtype)
+
+
+def scatter_kernel(
+    sizes,
+    grad_ref,
+    out_ref,
+    core_in,
+    core_sum,
+    col_in,
+    col_sum,
+    row_in,
+    row_sum,
+    wide_in,
+    other_wide_in,
+    other_wide_sum,
+    other_col_in,
+    other_col_sum,
+    other_row_in,
+    send_sem,
+    recv_sem,
+):
+    rows, cols, wides = sizes
+    row, col, wide, core = place(sizes)
+    row_peers = [((row + step) % rows, col, wide, core) for step in range(1, rows)]
+    col_peers = [(row, (col + step) % cols, wide, core) for step in range(1, cols)]
+    wide_peers = [(row, col, (wide + step) % wides, core) for step in range(1, wides)]
+    cross_peers = [(row, col, (wide + step) % wides, 1 - core) for step in range(wides)]
+    partner = cross_peers[0]
+    greet(
+        [device_at(sizes, *peer) for peer in row_peers + col_peers + wide_peers + cross_peers]
+    )
+    used = [0]
+    pending = []
+
+    def push(source, target, peer):
+        at = used[0]
+        used[0] += 1
+        return send(
+            source, target, send_sem.at[at], recv_sem.at[at], device_at(sizes, *peer)
+        )
+
+    def arrive(copies):
+        for copy in copies:
+            copy.wait_recv()
+        pending.extend(copies)
+
+    core_copies = [
+        push(grad_ref.at[:, :, 1 - core, half], core_in.at[half], partner) for half in range(2)
+    ]
+
+    def fold_core(half):
+        arrive([core_copies[half]])
+
+        def step(at, carry):
+            z = at // cols
+            y = at % cols
+            add_into(
+                core_sum.at[half, z, y],
+                grad_ref[z, y, core, half],
+                [core_in[half, z, y]],
+            )
+            return carry
+
+        lax.fori_loop(0, rows * cols, step, 0)
+
+    fold_core(0)
+    col_copies = [
+        push(core_sum.at[0, :, peer[1]], col_in.at[at], peer) for at, peer in enumerate(col_peers)
+    ]
+    fold_core(1)
+    other_wide_copies = [
+        push(core_sum.at[1, :, :, peer[2]], other_wide_in.at[at], peer)
+        for at, peer in enumerate(wide_peers)
+    ]
+    arrive(col_copies)
+
+    def fold_col(z, carry):
+        add_into(
+            col_sum.at[z], core_sum[0, z, col], [col_in[at, z] for at in range(cols - 1)]
+        )
+        return carry
+
+    lax.fori_loop(0, rows, fold_col, 0)
+    row_copies = [
+        push(col_sum.at[peer[0]], row_in.at[at], peer) for at, peer in enumerate(row_peers)
+    ]
+    arrive(other_wide_copies)
+
+    def fold_other_wide(at, carry):
+        z = at // cols
+        y = at % cols
+        add_into(
+            other_wide_sum.at[z, y],
+            core_sum[1, z, y, wide],
+            [other_wide_in[peer, z, y] for peer in range(wides - 1)],
+        )
+        return carry
+
+    lax.fori_loop(0, rows * cols, fold_other_wide, 0)
+    other_col_copies = [
+        push(other_wide_sum.at[:, peer[1]], other_col_in.at[at], peer)
+        for at, peer in enumerate(col_peers)
+    ]
+    arrive(other_col_copies)
+
+    def fold_other_col(z, carry):
+        add_into(
+            other_col_sum.at[z],
+            other_wide_sum[z, col],
+            [other_col_in[at, z] for at in range(cols - 1)],
+        )
+        return carry
+
+    lax.fori_loop(0, rows, fold_other_col, 0)
+    other_row_copies = [
+        push(other_col_sum.at[peer[0]], other_row_in.at[at], peer)
+        for at, peer in enumerate(row_peers)
+    ]
+    arrive(row_copies)
+    add_into(row_sum, col_sum[row], [row_in[at] for at in range(rows - 1)])
+    wide_copies = [
+        push(row_sum.at[peer[2]], wide_in.at[at], peer) for at, peer in enumerate(wide_peers)
+    ]
+    arrive(other_row_copies)
+    add_into(
+        out_ref.at[core, 1, wide],
+        other_col_sum[row],
+        [other_row_in[at] for at in range(rows - 1)],
+    )
+    last = [
+        push(out_ref.at[core, 1, wide], out_ref.at[core, 1, wide], peer)
+        for peer in wide_peers + cross_peers
+    ]
+    arrive(wide_copies)
+    add_into(
+        out_ref.at[core, 0, wide], row_sum[wide], [wide_in[at] for at in range(wides - 1)]
+    )
+    last += [
+        push(out_ref.at[core, 0, wide], out_ref.at[core, 0, wide], peer)
+        for peer in wide_peers + cross_peers
+    ]
+    arrive(last)
+    for copy in pending:
+        copy.wait_send()
+
+
+def quick_scatter(stacked, call_id):
+    sizes = grid_sizes()
+    rows, cols, wides = sizes
+    _, height, width = stacked.shape
+    part = height // (4 * wides)
+    messages = (
+        2 + 2 * (cols - 1) + 2 * (wides - 1) + 2 * (rows - 1) + 2 * (2 * wides - 1)
+    )
+    vmem = pl.BlockSpec(memory_space=pltpu.VMEM)
+    kind = stacked.dtype
+
+    def buffer(*shape):
+        return pltpu.VMEM((*shape, part, width), kind)
+
+    out = pl.pallas_call(
+        functools.partial(scatter_kernel, sizes),
+        out_shape=jax.ShapeDtypeStruct((2, 2, wides, part, width), kind),
+        in_specs=[vmem],
+        out_specs=vmem,
+        scratch_shapes=[
+            buffer(2, rows, cols, wides),
+            buffer(2, rows, cols, wides),
+            buffer(cols - 1, rows, wides),
+            buffer(rows, wides),
+            buffer(rows - 1, wides),
+            buffer(wides),
+            buffer(wides - 1),
+            buffer(wides - 1, rows, cols),
+            buffer(rows, cols),
+            buffer(cols - 1, rows),
+            buffer(rows),
+            buffer(rows - 1),
+            pltpu.SemaphoreType.DMA((messages,)),
+            pltpu.SemaphoreType.DMA((messages,)),
+        ],
+        compiler_params=pltpu.CompilerParams(
+            collective_id=call_id, has_side_effects=True, vmem_limit_bytes=56 << 20
+        ),
+        name="scatter_grads",
+    )(stacked.reshape(rows, cols, 2, 2, wides, part, width))
+    return out.reshape(height, width)
 
 
 def body(
@@ -261,18 +632,18 @@
         b_up,
     )
     vector_len = sum(vector.shape[0] for vector in vectors)
-    matrix_rows = w_roi.shape[0] + 4 * w_query.shape[0]
-    quantum = 16 * mod_size
+    pieces = (w_roi, w_query, w_key, w_value)
+    matrix_rows = sum(piece.shape[0] for piece in pieces)
+    quantum = 32 * mod_size
     vector_rows = -(-(matrix_rows + -(-vector_len // width)) // quantum) * quantum - matrix_rows
     packed_vectors = jnp.pad(
         jnp.concatenate(vectors), (0, vector_rows * width - vector_len)
     ).reshape(vector_rows, width)
-    pieces = (w_roi, w_query, w_key, w_value, w_out, packed_vectors)
-    first_full = gather_all(jnp.concatenate(pieces, 0))
+    first_full = quick_gather(jnp.concatenate([*pieces, packed_vectors], 0), 1)
     ff_parts = w_up.shape[1] // width
     up_blocks = w_up.reshape(w_up.shape[0], ff_parts, width).transpose(1, 0, 2)
     second_full = gather_all(
-        jnp.concatenate([up_blocks.reshape(-1, width), w_down], 0)
+        jnp.concatenate([up_blocks.reshape(-1, width), w_down, w_out], 0)
     )
 
     far_maps, far_boxes, far_grad = swapped(
@@ -311,10 +682,10 @@
     def unpack(full, start, count):
         return full[:, start : start + count].reshape(dp_size * count, width)
 
-    roi_weight, query_weight, key_weight, value_weight, out_weight = (
-        unpack(first_full, start, piece.shape[0]) for start, piece in zip(starts[:5], pieces[:5])
-    )
-    flat_vectors = first_full[:, starts[5] :].reshape(dp_size, vector_rows * width)
+    roi_weight, query_weight, key_weight, value_weight = (
+        unpack(first_full, start, piece.shape[0]) for start, piece in zip(starts, pieces)
+    )
+    flat_vectors = first_full[:, matrix_rows:].reshape(dp_size, vector_rows * width)
     full_vectors = []
     at = 0
     for vector in vectors:
@@ -343,6 +714,7 @@
         .reshape(width, ff_parts * width)
     )
     down_weight = unpack(second_full, up_rows, w_down.shape[0])
+    out_weight = unpack(second_full, up_rows + w_down.shape[0], w_out.shape[0])
 
     projected = product(pooled, roi_weight)
     stats = jnp.stack(
@@ -352,7 +724,7 @@
             jnp.broadcast_to(jnp.sum(roi_mask), (width,)),
         ]
     )
-    stats = total_sum(stats)
+    stats = total_sum(stats, 2)
     number = stats[2:3]
     average = stats[0:1] / number
     variance = stats[1:2] / number - average * average
@@ -438,49 +810,14 @@
     ).reshape(page_count, slots, width)
     grad_text = grad_rows[:, :text_slots]
     grad_roi = grad_rows[:, text_slots:].reshape(page_count * roi_slots, width)
-    sums = total_sum(jnp.stack([jnp.sum(grad_roi, 0), jnp.sum(grad_roi * standard, 0)]))
     grad_w_query = inner_rows(rows_in, grad_queries).astype(bf16)
     grad_b_query = jnp.sum(grad_queries.astype(f32), 0)
     grad_w_key = inner_rows(rows_in, grad_keys).astype(bf16)
     grad_w_value = inner_rows(rows_in, grad_values).astype(bf16)
     grad_b_value = jnp.sum(grad_values.astype(f32), 0)
-    sum_grad = sums[0:1]
-    sum_scaled = sums[1:2]
-    grad_projected = (
-        inv_std
-        * (
-            grad_roi * norm_gain
-            - roi_mask * norm_gain * (sum_grad + standard * sum_scaled) / number
-        )
-    ).astype(bf16)
-    grad_w_roi = inner_rows(pooled, grad_projected).astype(bf16)
-    grad_pooled = (
-        outer_cols(grad_projected, roi_weight)
-        .astype(bf16)
-        .reshape(page_count, roi_slots, 2 * channels)
-    )
-    own_pooled = swapped(grad_pooled, "mod", top_bit)
-    own_coarse, own_fine, own_coarse_area, own_fine_area = box_masks(boxes)
-
-    def spread(mask, grad, area):
-        return jnp.einsum(
-            "prc,prf->pcf",
-            mask.astype(bf16),
-            (grad.astype(f32) / area).astype(bf16),
-            preferred_element_type=f32,
-        )
-
-    grad_maps = jnp.concatenate(
-        [
-            spread(own_coarse, own_pooled[..., :channels], own_coarse_area),
-            spread(own_fine, own_pooled[..., channels:], own_fine_area),
-        ],
-        1,
-    )
-
     grad_vectors = (
-        jnp.zeros_like(grad_b_out),
-        jnp.zeros_like(grad_b_out),
+        jnp.sum(grad_roi * standard, 0),
+        jnp.sum(grad_roi, 0),
         grad_b_query,
         grad_b_value,
         grad_b_out,
@@ -489,34 +826,63 @@
         grad_b_down,
         grad_ln2_gain,
         grad_ln2_bias,
-        grad_b_up,
-    )
-    vector_stack = jnp.concatenate(
-        [vector.astype(bf16).reshape(dp_size, -1) for vector in grad_vectors], 1
-    )
-    vector_stack = jnp.pad(
-        vector_stack, ((0, 0), (0, vector_rows * width - vector_len))
-    ).reshape(dp_size, vector_rows, width)
-    first_share = scatter_sum(
+    )
+    sums = total_sum(
+        jnp.concatenate(
+            [vector[None] for vector in grad_vectors] + [grad_b_up.reshape(ff_parts, width)], 0
+        ),
+        3,
+    )
+    sum_scaled = sums[0:1]
+    sum_grad = sums[1:2]
+    grad_projected = (
+        inv_std
+        * (
+            grad_roi * norm_gain
+            - roi_mask * norm_gain * (sum_grad + standard * sum_scaled) / number
+        )
+    ).astype(bf16)
+    grad_w_roi = inner_rows(pooled, grad_projected).astype(bf16)
+    grad_pooled = (
+        outer_cols(grad_projected, roi_weight)
+        .astype(bf16)
+        .reshape(page_count, roi_slots, 2 * channels)
+    )
+    own_pooled = swapped(grad_pooled, "mod", top_bit)
+    own_coarse, own_fine, own_coarse_area, own_fine_area = box_masks(boxes)
+
+    def spread(mask, grad, area):
+        return jnp.einsum(
+            "prc,prf->pcf",
+            mask.astype(bf16),
+            (grad.astype(f32) / area).astype(bf16),
+            preferred_element_type=f32,
+        )
+
+    grad_maps = jnp.concatenate(
+        [
+            spread(own_coarse, own_pooled[..., :channels], own_coarse_area),
+            spread(own_fine, own_pooled[..., channels:], own_fine_area),
+        ],
+        1,
+    )
+
+    first_share = quick_scatter(
         jnp.concatenate(
             [
                 grad.reshape(dp_size, -1, width)
                 for grad in (grad_w_roi, grad_w_query, grad_w_key, grad_w_value, grad_w_out)
-            ]
-            + [vector_stack],
+            ],
             1,
-        )
+        ),
+        4,
     ).astype(f32)
-    own_w_roi, own_w_query, own_w_key, own_w_value, own_w_out = (
-        first_share[start : start + piece.shape[0]]
-        for start, piece in zip(starts[:5], pieces[:5])
-    )
-    flat_share = first_share[starts[5] :].reshape(-1)
-    vector_shares = []
+    own_matrices = []
     at = 0
-    for vector in vectors:
-        vector_shares.append(flat_share[at : at + vector.shape[0]])
-        at += vector.shape[0]
+    for piece in (*pieces, w_out):
+        own_matrices.append(first_share[at : at + piece.shape[0]])
+        at += piece.shape[0]
+    own_w_roi, own_w_query, own_w_key, own_w_value, own_w_out = own_matrices
     own_w_up = (
         second_share[:up_rows]
         .reshape(ff_parts, w_up.shape[0], width)
@@ -525,33 +891,40 @@
         .astype(f32)
     )
     own_w_down = second_share[up_rows:].astype(f32)
+    my_dp = lax.axis_index("dp")
     share_len = width // dp_size
-    share_start = lax.axis_index("dp") * share_len
-    gain_share = lax.dynamic_slice_in_dim(sums[1], share_start, share_len, 0)
-    bias_share = lax.dynamic_slice_in_dim(sums[0], share_start, share_len, 0)
+    vector_share = lax.dynamic_slice_in_dim(
+        sums[: len(grad_vectors)], my_dp * share_len, share_len, 1
+    )
+    up_share = lax.dynamic_slice_in_dim(
+        sums[len(grad_vectors) : len(grad_vectors) + ff_parts].reshape(-1),
+        my_dp * b_up.shape[0],
+        b_up.shape[0],
+        0,
+    )
     return (
         out_text,
         out_roi,
         grad_text,
         grad_maps,
         own_w_roi,
-        gain_share,
-        bias_share,
+        vector_share[0],
+        vector_share[1],
         own_w_query,
         own_w_key,
         own_w_value,
-        vector_shares[2],
-        vector_shares[3],
+        vector_share[2],
+        vector_share[3],
         own_w_out,
-        vector_shares[4],
-        vector_shares[5],
-        vector_shares[6],
+        vector_share[4],
+        vector_share[5],
+        vector_share[6],
         own_w_up,
-        vector_shares[10],
+        up_share,
         own_w_down,
-        vector_shares[7],
-        vector_shares[8],
-        vector_shares[9],
+        vector_share[7],
+        vector_share[8],
+        vector_share[9],
     )
 
 

time: 556 us -> 450 us (0.81)
  Pallas kernels: 44.4 us -> 196 us
  waiting for transfers between devices: 196 us -> 68 us
  blocking collectives: 91.2 us -> 0 us
  local copies, waits for them, and re-layouts: 85.6 us -> 58.7 us
  other arithmetic: 28.4 us -> 22 us
    pallas_call x0 -> x4, Pallas kernels: none -> 151 us  [the longest x1 55.7 us: quick_scatter(): pl.pallas_call(functools.partial(scatter_kernel, sizes), out_shape=jax.Sh...]
    psum x2 -> x0, blocking collectives: 82.5 us -> none  [total_sum(): return lax.psum(stats, BOTH)]
    reduce_scatter x2 -> x1, waiting for transfers between devices: 129 us -> 56.4 us  [scatter_sum(): lax.psum_scatter(stacked.reshape(dp_size * rows, width), BOTH, scatter_di...]
    all_gather x2 -> x1, waiting for transfers between devices: 55.3 us -> 0.02 us  [gather_all(): full = lax.all_gather(mine, BOTH, axis=0, tiled=True)]
    unnamed x209 -> x195, local copies, waits for them, and re-layouts: 28.6 us -> 16.4 us
    all_gather x1 -> x0, blocking collectives: 8.71 us -> none  [scatter_sum(): return lax.all_gather(part, 'mod', axis=0, tiled=True)]
    concatenate x1, local copies, waits for them, and re-layouts: 7.45 us -> 0.09 us  [body(): jnp.concatenate(vectors)]
    all_gather x1, waiting for transfers between devices: 6.13 us -> 0.01 us  [scatter_sum(): return lax.all_gather(part, 'mod', axis=0, tiled=True)]
  transfers between devices with their start and end apart: 10 -> 8, of which waited for: 5 -> 3; matrix products, arithmetic and copies ran while one was open for 15% -> 13% of each run, Pallas kernels for 8% -> 44%
where the time goes in v2:
time: 450 us; the launch traced here: 443 us
  Pallas kernels  196 us (44%)
  matrix products  75.1 us (17%)
  waiting for transfers between devices  68 us (15%)
  local copies, waits for them, and re-layouts  58.7 us (13%)
  other arithmetic  22 us (5%)
  between operations  15.8 us (4%)
  starting transfers between devices  8.23 us (2%)
    reduce_scatter x1, waiting for transfers between devices, scatter_sum(): lax.psum_scatter(stacked.reshape(dp_size * rows, width), BOTH, scatter_di...  56.4 us
    pallas_call x1, Pallas kernels, quick_scatter(): pl.pallas_call(functools.partial(scatter_kernel, sizes), out_shape=jax.Sh...  55.7 us
    pallas_call x1, Pallas kernels, quick_gather(): pl.pallas_call(functools.partial(gather_kernel, sizes), out_shape=jax.Sha...  49.5 us
    pallas_call x2, Pallas kernels, total_sum(): pl.pallas_call(functools.partial(total_kernel, mod_size, dp_size), out_sh...  45.7 us
    pallas_call x2, Pallas kernels, attention_call(): pl.pallas_call(kernel, out_shape=tuple((jax.ShapeDtypeStruct((rows, width...  44.7 us
    dot_general x7, matrix products, outer_cols(): lax.dot_general(left_mat, right_mat, (((1,), (1,)), ((), ())), preferred_...  27.9 us
    dot_general x7, matrix products, inner_rows(): lax.dot_general(left_mat, right_mat, (((0,), (0,)), ((), ())), preferred_...  23.6 us
    dot_general x7, matrix products, product(): return jnp.dot(left_mat, right_mat, preferred_element_type=jnp.float32)  22.4 us
  transfers between devices with their start and end apart: 8, of which 3 were waited for; matrix products, arithmetic and copies ran while one was open for 13% of the time, Pallas kernels for 44%

profile of v2, /device:TPU:0, one launch (start us, length us, event | category | flops | bytes accessed | tf_op | source)
XLA Modules:
  0.0 443.4 jit_solution(14747364661592022946)
XLA Ops:
  10.1 4.0 collective-permute-start
  16.7 49.5 %gather_weights.1 = bf16[4,2,2,2,2,48,768]{6,5,4,3,2,1,0:T(8,128)(2,1)S(1)} custom-call(bf16[2,2,2,48,768]{4,3,2,1,0:T(8,128)(2,1)S(1)} %bitcast.157), custom_call_target="tpu_custom_call" | custom-call | tf_op jit(solution)/shard_map/gather_weights/pallas_call | solution.py:368
  73.8 19.8 %total_2.1 = f32[8,768]{1,0:T(8,128)S(1)} custom-call(f32[8,768]{1,0:T(8,128)S(1)} %pad.13.stats_ref), custom_call_target="tpu_custom_call" | custom-call | tf_op jit(solution)/shard_map/total_2/pallas_call | solution.py:287
  98.7 18.6 %shard_map.399 = (bf16[1024,768]{1,0:T(8,128)(2,1)S(1)}, f32[1024,768]{1,0:T(8,128)S(1)}) custom-call(s32[2,2]{1,0:T(2,128)S(1)} %copy.62.counts_ref, bf16[1024,768]{1,0:T(8,128)(2,1)S(1)} %add_convert_fusion.1.query_ref, bf16[1024,768]{1,0:T(8,128)(2,1)S(1)} %convolution_convert_fusion.3.key_ref, bf16[1024,768]{1,0:T(8,128)(2,1)S(1)} %add_convert_fusion.value_ref), custom_call_target="tpu_custom_call" | custom-call | flops 1610612736 | bytes 7864320 | tf_op jit(solution)/shard_map/pallas_call | solution.py:169
  122.1 6.8 %fusion.35 = (bf16[8,384,768]{2,1,0:T(8,128)(2,1)}, bf16[8,384,768]{2,1,0:T(8,128)(2,1)S(1)}) fusion(bf16[8,864,768]{2,1,0:T(8,128)(2,1)} %bitcast.166), kind=kLoop, calls=%fused_computation.201 | loop fusion | bytes 18874368 | tf_op jit(solution)/shard_map/slice | solution.py:683
  128.9 2.9 fusion.38
  132.3 3.6 copy.58
  137.0 9.5 %multiply_convert_fusion.1 = (bf16[1024,3072]{1,0:T(8,128)(2,1)S(1)}, f32[1024,3072]{1,0:T(8,128)}) fusion(f32[3072]{0:T(1024)S(1)} %reshape.426, bf16[768,3072]{1,0:T(8,128)(2,1)S(1)} %bitcast.169, f32[1024,768]{1,0:T(8,128)S(1)} %get-tuple-element.113, f32[768]{0:T(1024)S(1)} %reshape.425, f32[768]{0:T(1024)S(1)} %reshape.424, ...), kind=kOutput, calls=%fused_computation.8 | convolution fusion | flops 4854644736 | bytes 26765312 | tf_op jit(solution)/shard_map/dot_general | solution.py:28
  146.6 5.5 %fusion.39 = (f32[1024]{0:T(1024)S(1)}, f32[1024,768]{1,0:T(8,128)S(1)}) fusion(f32[768]{0:T(1024)S(1)} %reshape.427, bf16[1024,3072]{1,0:T(8,128)(2,1)S(1)} %get-tuple-element.114, bf16[3072,768]{1,0:T(8,128)(2,1)S(1)} %bitcast.173, f32[768]{0:T(1024)S(1)} %reshape.425, f32[768]{0:T(1024)S(1)} %reshape.424, f32[1024]{0:T(1024)S(1)} %add_rsqrt_fusion.1, ...), kind=kOutput, calls=%fused_computation.205 | convolution fusion | flops 4837342208 | bytes 17323008 | tf_op jit(solution)/shard_map/dot_general | solution.py:28
  156.6 7.1 %convolution_convert_fusion = bf16[3072,768]{1,0:T(8,128)(2,1)} fusion(bf16[1024,3072]{1,0:T(8,128)(2,1)S(1)} %get-tuple-element.114, f32[1024,768]{1,0:T(8,128)S(1)} %get-tuple-element.54), kind=kOutput, calls=%fused_computation.11 | convolution fusion | flops 4834983936 | bytes 14155776 | tf_op jit(solution)/shard_map/dot_general | solution.py:32
  163.7 11.8 %convert_reduce_fusion = (f32[3072]{0:T(1024)S(1)}, bf16[1024,3072]{1,0:T(8,128)(2,1)S(1)}) fusion(f32[1024,3072]{1,0:T(8,128)} %get-tuple-element.115, f32[3072]{0:T(1024)S(1)} %reshape.426, bf16[3072,768]{1,0:T(8,128)(2,1)S(1)} %bitcast.174, f32[1024,768]{1,0:T(8,128)S(1)} %get-tuple-element.54), kind=kOutput, calls=%fused_computation.6 | convolution fusion | flops 4879807488 | bytes 26763264 | tf_op jit(solution)/shard_map/dot_general | solution.py:38
  175.5 2.6 copy-done.85
  178.1 8.3 %convolution_convert_fusion.1 = bf16[768,3072]{1,0:T(8,128)(2,1)} fusion(bf16[1024,3072]{1,0:T(8,128)(2,1)S(1)} %get-tuple-element.120, f32[1024,768]{1,0:T(8,128)S(1)} %get-tuple-element.113, f32[768]{0:T(1024)S(1)} %reshape.425, f32[768]{0:T(1024)S(1)} %reshape.424, f32[1024]{0:T(1024)S(1)} %add_rsqrt_fusion.1, f32[1024]{0:T(1024)S(1)} %broadcast_multiply_fusion.4), kind=kOutput, calls=%fused_computation.12 | convolution fusion | flops 4838129664 | bytes 14170112 | tf_op jit(solution)/shard_map/dot_general | solution.py:32
  186.4 9.8 %reshape.413 = bf16[8,96,4,768]{3,2,1,0:T(4,128)(2,1)} reshape(bf16[768,3072]{1,0:T(8,128)(2,1)} %convolution_convert_fusion.1) | data formatting | bytes 9437184 | tf_op jit(solution)/shard_map/reshape | solution.py:779
  196.2 3.4 copy.59
  199.8 3.9 pad_maximum_fusion
  208.1 10.0 %multiply_reduce_fusion.1 = (f32[768]{0:T(1024)S(1)}, f32[1024]{0:T(1024)S(1)}, f32[1024]{0:T(1024)S(1)}, f32[768]{0:T(1024)S(1)}, f32[1024,768]{1,0:T(8,128)S(1)}) fusion(f32[1024,768]{1,0:T(8,128)S(1)} %copy-done.15, f32[1024]{0:T(1024)S(1)} %add_rsqrt_fusion.1, f32[1024]{0:T(1024)S(1)} %broadcast_multiply_fusion.4, f32[768]{0:T(1024)S(1)} %reshape.424, ...), kind=kOutput, calls=%fused_computation.16 | convolution fusion | flops 4839698432 | bytes 20472832 | tf_op jit(solution)/shard_map/dot_general | solution.py:38
  223.7 26.1 %shard_map.400 = (bf16[1024,768]{1,0:T(8,128)(2,1)S(1)}, bf16[1024,768]{1,0:T(8,128)(2,1)S(1)}, bf16[1024,768]{1,0:T(8,128)(2,1)S(1)}) custom-call(s32[2,2]{1,0:T(2,128)S(1)} %copy.62.counts_ref, bf16[1024,768]{1,0:T(8,128)(2,1)S(1)} %copy-done.13, bf16[1024,768]{1,0:T(8,128)(2,1)S(1)} %copy-done.9, bf16[1024,768]{1,0:T(8,128)(2,1)S(1)} %copy-done.11, ...), custom_call_target="tpu_custom_call" | custom-call | flops 4026531840 | bytes 12582912 | tf_op jit(solution)/shard_map/pallas_call | solution.py:169
  257.9 25.9 %total_3.1 = f32[16,768]{1,0:T(8,128)S(1)} custom-call(f32[16,768]{1,0:T(8,128)S(1)} %pad.14.stats_ref), custom_call_target="tpu_custom_call" | custom-call | tf_op jit(solution)/shard_map/total_3/pallas_call | solution.py:287
  295.1 2.5 convolution_convert_fusion.4
  297.7 56.4 %reduce-scatter.2.cloned.1.call-done = bf16[192,768]{1,0:T(8,128)(2,1)} async-done(((bf16[6144,768]{1,0:T(8,128)(2,1)}), bf16[192,768]{1,0:T(8,128)(2,1)}) %reduce-scatter.2.cloned.1.call-update) | async-done | bytes 294928 | tf_op jit(solution)/shard_map/reduce_scatter | solution.py:199
  356.4 55.7 %scatter_grads.1 = bf16[2,2,2,56,768]{4,3,2,1,0:T(8,128)(2,1)} custom-call(bf16[4,2,2,2,2,56,768]{6,5,4,3,2,1,0:T(8,128)(2,1)} %bitcast.44.grad_ref), custom_call_target="tpu_custom_call" | custom-call | tf_op jit(solution)/shard_map/scatter_grads/pallas_call | solution.py:551
  419.0 4.8 %collective-permute-done.4 = bf16[2,128,512]{2,1,0:T(8,128)(2,1)S(1)} collective-permute-done((bf16[2,128,512]{2,1,0:T(8,128)(2,1)S(1)}, bf16[2,128,512]{2,1,0:T(8,128)(2,1)S(1)}, u32[]{:S(2)}, u32[]{:S(2)}) %collective-permute-start.4) | collective-permute-done | bytes 262176 | tf_op jit(solution)/shard_map/ppermute | solution.py:24
  425.4 6.6 %collective-permute-done.2 = bf16[2,128,768]{2,1,0:T(8,128)(2,1)S(1)} collective-permute-done((bf16[2,128,768]{2,1,0:T(8,128)(2,1)S(1)}, bf16[2,128,768]{2,1,0:T(8,128)(2,1)S(1)}, u32[]{:S(2)}, u32[]{:S(2)}) %collective-permute-start.2) | collective-permute-done | bytes 393248 | tf_op jit(solution)/shard_map/ppermute | solution.py:24
  (318 shorter events, 72.5 us)
Async XLA Ops:
  7.4 112.3 %all-gather.3.cloned.1.call-start = ((), (), s32[]{:S(2)}) async-start(), calls=%async_computation.1 | async-start | bytes 10948608 | tf_op jit(solution)/shard_map/all_gather | solution.py:193
  10.1 344.0 %reduce-scatter.2.cloned.1.call-start = ((), (), s32[]{:S(2)}) async-start(), calls=%async_computation.2 | async-start | bytes 9732096 | tf_op jit(solution)/shard_map/reduce_scatter | solution.py:199
  10.1 60.9 %collective-permute-start = (s32[2,128,4]{1,2,0:T(4,128)S(1)}, s32[2,128,4]{1,2,0:T(4,128)S(1)}, u32[]{:S(2)}, u32[]{:S(2)}) collective-permute-start(s32[2,128,4]{1,2,0:T(4,128)S(1)} %copy-done.46), channel_id=1, source_target_pairs={{0,2},{2,0},{1,3},{3,1},{4,6},{6,4},{5,7},{7,5},{8,10},{10,8},{9,1... | collective-permute-start | bytes 12296 | tf_op jit(solution)/shard_map/ppermute | solution.py:24
  14.1 58.5 %collective-permute-start.1 = (bf16[2,320,256]{2,1,0:T(8,128)(2,1)S(1)}, bf16[2,320,256]{2,1,0:T(8,128)(2,1)S(1)}, u32[]{:S(2)}, u32[]{:S(2)}) collective-permute-start(bf16[2,320,256]{2,1,0:T(8,128)(2,1)S(1)} %copy-done.84), channel_id=1, source_target_pairs={{0,2},{2,0},{1,3},{3,1},{4,6},{6,4},{5,7},{7,5},{8,10},{10,8},{9,1... | collective-permute-start | bytes 983048 | tf_op jit(solution)/shard_map/ppermute | solution.py:24
  14.2 104.7 %collective-permute-start.3 = (bf16[2,128,768]{2,1,0:T(8,128)(2,1)}, bf16[2,128,768]{2,1,0:T(8,128)(2,1)S(1)}, u32[]{:S(2)}, u32[]{:S(2)}) collective-permute-start(bf16[2,128,768]{2,1,0:T(8,128)(2,1)} %param.47), channel_id=1, source_target_pairs={{0,2},{2,0},{1,3},{3,1},{4,6},{6,4},{5,7},{7,5},{8,10},{10,8},{9,1... | collective-permute-start | bytes 1179656 | tf_op jit(solution)/shard_map/ppermute | solution.py:24
  69.4 24.5 %copy-start.23 = (bf16[8,96,768]{2,1,0:T(8,128)(2,1)}, bf16[8,96,768]{2,1,0:T(8,128)(2,1)S(1)}, u32[]{:S(2)}) copy-start(bf16[8,96,768]{2,1,0:T(8,128)(2,1)S(1)} %get-tuple-element.59) | copy-start | bytes 3538948
  69.5 24.3 %copy-start.27 = (bf16[8,64,768]{2,1,0:T(8,128)(2,1)}, bf16[8,64,768]{2,1,0:T(8,128)(2,1)S(1)}, u32[]{:S(2)}) copy-start(bf16[8,64,768]{2,1,0:T(8,128)(2,1)S(1)} %slice.250) | copy-start | bytes 2359300
  72.6 21.2 %copy-start.33 = (bf16[2,384,768]{2,1,0:T(8,128)(2,1)S(1)}, bf16[2,384,768]{2,1,0:T(8,128)(2,1)}, u32[]{:S(2)}) copy-start(bf16[2,384,768]{2,1,0:T(8,128)(2,1)} %param.24) | copy-start | bytes 3538948
  73.7 19.9 %copy-start.19 = (f32[256,768]{1,0:T(8,128)}, f32[256,768]{1,0:T(8,128)S(1)}, u32[]{:S(2)}) copy-start(f32[256,768]{1,0:T(8,128)S(1)} %get-tuple-element.111) | copy-start | bytes 2359300
  98.6 18.6 %copy-start.8 = (bf16[1024,768]{1,0:T(8,128)(2,1)}, bf16[1024,768]{1,0:T(8,128)(2,1)S(1)}, u32[]{:S(2)}) copy-start(bf16[1024,768]{1,0:T(8,128)(2,1)S(1)} %convolution_convert_fusion.3.key_ref) | copy-start | bytes 4718596
  98.6 20.3 %copy-start.18 = (bf16[2,384,768]{2,1,0:T(8,128)(2,1)S(1)}, bf16[2,384,768]{2,1,0:T(8,128)(2,1)}, u32[]{:S(2)}) copy-start(bf16[2,384,768]{2,1,0:T(8,128)(2,1)} %param.46) | copy-start | bytes 3538948
  131.7 43.8 %copy-start.14 = (f32[1024,768]{1,0:T(8,128)}, f32[1024,768]{1,0:T(8,128)S(1)}, u32[]{:S(2)}) copy-start(f32[1024,768]{1,0:T(8,128)S(1)} %get-tuple-element.113) | copy-start | bytes 9437188
  186.4 13.2 %slice-start.2 = ((s8[4718592]{0:T(1024)(128)(4,1)}), s8[524288]{0:T(1024)(128)(4,1)S(1)}, s32[]{:S(2)}) async-start(s8[4718592]{0:T(1024)(128)(4,1)} %bitcast.175), calls=%async_computation.6 | async-start | bytes 1048576
  203.8 228.3 %all-gather.5.cloned.1.call-start = ((), (), s32[]{:S(2)}) async-start(), calls=%async_computation.3 | async-start | bytes 1474560 | tf_op jit(solution)/shard_map/all_gather | solution.py:202
  219.3 33.8 %copy-start.16 = (f32[1024,768]{1,0:T(8,128)}, f32[1024,768]{1,0:T(8,128)S(1)}, u32[]{:S(2)}) copy-start(f32[1024,768]{1,0:T(8,128)S(1)} %get-tuple-element.56) | copy-start | bytes 9437188
  223.7 26.2 %copy-start.37 = (bf16[8,96,768]{2,1,0:T(8,128)(2,1)S(1)}, bf16[8,96,768]{2,1,0:T(8,128)(2,1)}, u32[]{:S(2)}) copy-start(bf16[8,96,768]{2,1,0:T(8,128)(2,1)} %get-tuple-element.61) | copy-start | bytes 3538948
  257.8 29.4 %copy-start.32 = (bf16[2,512,768]{2,1,0:T(8,128)(2,1)S(1)}, bf16[2,512,768]{2,1,0:T(8,128)(2,1)}, u32[]{:S(2)}) copy-start(bf16[2,512,768]{2,1,0:T(8,128)(2,1)} %copy-done.30) | copy-start | bytes 4718596
  295.1 59.0 %copy-start.39 = (bf16[768,768]{1,0:T(8,128)(2,1)S(1)}, bf16[768,768]{1,0:T(8,128)(2,1)}, u32[]{:S(2)}) copy-start(bf16[768,768]{1,0:T(8,128)(2,1)} %convolution_convert_fusion.5) | copy-start | bytes 3538948
  297.7 57.6 %copy-start.40 = (bf16[768,768]{1,0:T(8,128)(2,1)S(1)}, bf16[768,768]{1,0:T(8,128)(2,1)}, u32[]{:S(2)}) copy-start(bf16[768,768]{1,0:T(8,128)(2,1)} %convolution_convert_fusion.4) | copy-start | bytes 3538948
  356.4 57.8 %copy-start.26 = (bf16[256,768]{1,0:T(8,128)(2,1)S(1)}, bf16[256,768]{1,0:T(8,128)(2,1)}, u32[]{:S(2)}) copy-start(bf16[256,768]{1,0:T(8,128)(2,1)} %copy-done.25) | copy-start | bytes 1179652
  356.4 57.8 %copy-start.28 = (bf16[8,64,768]{2,1,0:T(8,128)(2,1)S(1)}, bf16[8,64,768]{2,1,0:T(8,128)(2,1)}, u32[]{:S(2)}) copy-start(bf16[8,64,768]{2,1,0:T(8,128)(2,1)} %copy-done.27) | copy-start | bytes 2359300
  412.1 11.7 %copy-start.60 = (s32[2,128,1]{1,2,0:T(1,128)S(1)}, s32[2,128,1]{1,2,0:T(1,128)}, u32[]{:S(2)}) copy-start(s32[2,128,1]{1,2,0:T(1,128)} %copy-done.59) | copy-start | bytes 3076
  414.6 9.2 %collective-permute-start.4 = (bf16[2,128,512]{2,1,0:T(8,128)(2,1)S(1)}, bf16[2,128,512]{2,1,0:T(8,128)(2,1)S(1)}, u32[]{:S(2)}, u32[]{:S(2)}) collective-permute-start(bf16[2,128,512]{2,1,0:T(8,128)(2,1)S(1)} %bitcast.207), channel_id=1, source_target_pairs={{0,2},{2,0},{1,3},{3,1},{4,6},{6,4},{5,7},{7,5},{8,10},{10,8},{9,1... | collective-permute-start | bytes 786440 | tf_op jit(solution)/shard_map/ppermute | solution.py:24
  415.4 16.7 %collective-permute-start.2 = (bf16[2,128,768]{2,1,0:T(8,128)(2,1)S(1)}, bf16[2,128,768]{2,1,0:T(8,128)(2,1)S(1)}, u32[]{:S(2)}, u32[]{:S(2)}) collective-permute-start(bf16[2,128,768]{2,1,0:T(8,128)(2,1)S(1)} %copy-done.41), channel_id=1, source_target_pairs={{0,2},{2,0},{1,3},{3,1},{4,6},{6,4},{5,7},{7,5},{8,10},{10,8},{9,1... | collective-permute-start | bytes 1179656 | tf_op jit(solution)/shard_map/ppermute | solution.py:24
  (74 other events, 466.5 us)
Sparse Core Ops, SparseCore 0:
  11.7 106.5 all-gather.2
  203.9 150.1 reduce-scatter.1
  355.7 18.5 all-gather.4
